TPU v7x, 32 devices: a whole 2x2x4 slice. The times are simulated.
32 devices in a mesh: dp: 16 (over z, y, x), tensor: 2 (over core).
Axes of the slice: x: 2, y: 2, z: 4, core: 2. Of those that a mesh axis runs over, the one named last changes fastest.
Arguments:
- tokens: bfloat16 [2048, 1792], P('dp'), may hold values from -6 to 6
- targets: bfloat16 [2048, 1792], P('dp'), may hold values from -6 to 6
- live_mask: int32 [2048], P('dp'), may hold values from 0 to 1, as said below
- up_weight: bfloat16 [1792, 7168], P('dp', 'tensor'), may hold values from -0.125 to 0.125
- down_weight: bfloat16 [1792, 7168], P('dp', 'tensor'), may hold values from -0.0625 to 0.0625
- probe_rows: int32 [1792], replicated, may hold values from 0 to 16777215
- probe_cols: int32 [7168], P('tensor'), may hold values from 0 to 16777215
- moment: float32 [1792, 512], P('dp', 'tensor'), may hold values from 0.01 to 1
Outputs:
- hess_diag: float32 [1792, 512], P('dp', 'tensor')
- second_moment: float32 [1792, 512], P('dp', 'tensor')
- mean_loss: float32 [], replicated
Inputs may be any that keep to these rules, and one draw needn't show every extreme that they name: In every aligned block of 128 tokens the first token has live_mask 1.
All inputs are finite; a program needn't handle non-finite values.
Results may differ from a plain program's by a relative error of at most 0.0023.
Values may be sent and summed in bfloat16 or wider, within the bound.
A program may use at most 128 MiB of HBM per device.

v0:
```python
import jax
import jax.numpy as jnp
from jax import lax
from jax.sharding import PartitionSpec as P

BLOCK = 14


gelu_coef = 0.7978845608028654
cubic_coef = 0.044715
beta_two = 0.999


def probe_signs(row_keys, col_keys):
    hashed = jnp.bitwise_xor(row_keys[:, None] * 747796405, col_keys[None, :])
    hashed = jnp.bitwise_xor(hashed, jnp.right_shift(hashed, 15) & 131071)
    hashed = hashed * 695872825
    hashed = jnp.bitwise_xor(hashed, jnp.right_shift(hashed, 13) & 524287)
    hashed = hashed * 739982445
    hashed = jnp.bitwise_xor(hashed, jnp.right_shift(hashed, 16) & 65535)
    parity = jnp.right_shift(hashed, 11) & 1
    return (2 * parity - 1).astype(jnp.bfloat16)


def gelu_parts(preact):
    tanh_arg = gelu_coef * (preact + cubic_coef * preact * preact * preact)
    tanh_val = jnp.tanh(tanh_arg)
    sech_sq = 1.0 - tanh_val * tanh_val
    arg_slope = gelu_coef * (1.0 + 3.0 * cubic_coef * preact * preact)
    arg_curve = gelu_coef * 6.0 * cubic_coef * preact
    gelu_value = 0.5 * preact * (1.0 + tanh_val)
    gelu_slope = 0.5 * (1.0 + tanh_val) + 0.5 * preact * sech_sq * arg_slope
    gelu_curve = sech_sq * (
        arg_slope - preact * tanh_val * arg_slope * arg_slope + 0.5 * preact * arg_curve
    )
    return (gelu_value, gelu_slope, gelu_curve)


def body(tokens, targets, live_mask, up_weight, down_weight, probe_rows, probe_cols, moment):
    tok_count = tokens.shape[0]
    ff_local = up_weight.shape[1]
    own_rows = up_weight.shape[0]
    tensor_count = lax.axis_size("tensor")
    live_rows = live_mask.astype(jnp.float32)
    local_count = jnp.sum(live_rows) * (1.0 / tensor_count)
    all_signs = probe_signs(probe_rows, probe_cols)
    total_count = lax.psum(local_count, ("dp", "tensor"))
    columns = tokens
    sign_rows = all_signs
    joined = jnp.concatenate(
        [lax.all_gather(up_weight, "dp", axis=0, tiled=True), sign_rows], axis=1
    )
    both_pre = jnp.dot(columns, joined, preferred_element_type=jnp.float32)
    preact = both_pre[:, :ff_local]
    tangent = both_pre[:, ff_local:]
    full_down = lax.all_gather(down_weight, "dp", axis=0, tiled=True)
    gelu_value, gelu_slope, gelu_curve = gelu_parts(preact)
    hidden = gelu_value.astype(jnp.bfloat16)
    hidden_dir = (gelu_slope * tangent).astype(jnp.bfloat16)
    stacked = jnp.concatenate([hidden, hidden_dir], axis=0)
    projected = jnp.einsum("tf,df->td", stacked, full_down, preferred_element_type=jnp.float32)
    outputs, out_dir = lax.psum((projected[:tok_count], projected[tok_count:]), "tensor")
    diff = outputs - targets.astype(jnp.float32)
    weighted = live_rows[:, None] * diff
    local_loss = jnp.sum(weighted * diff) * (1.0 / tensor_count)
    residual = weighted.astype(jnp.bfloat16)
    residual_dir = (live_rows[:, None] * out_dir).astype(jnp.bfloat16)
    back_prod = jnp.dot(
        jnp.concatenate([residual, residual_dir], axis=0),
        full_down,
        preferred_element_type=jnp.float32,
    )
    grad_h = back_prod[:tok_count]
    grad_dir = back_prod[tok_count:]
    chain_grad = (grad_dir * gelu_slope + grad_h * gelu_curve * tangent).astype(jnp.bfloat16)
    columns = tokens
    product = jnp.einsum("tr,tf->rf", columns, chain_grad, preferred_element_type=jnp.float32)
    sign_rows = all_signs
    hutch_terms = sign_rows.astype(jnp.float32) * product
    own_share = lax.psum_scatter(
        hutch_terms.reshape(own_rows * lax.axis_size("dp"), ff_local // BLOCK, BLOCK).mean(axis=-1),
        "dp",
        scatter_dimension=0,
        tiled=True,
    )
    loss_sum = lax.psum(local_loss, ("dp", "tensor"))
    hess_diag = own_share / total_count
    second_moment = beta_two * moment + (1.0 - beta_two) * hess_diag * hess_diag
    mean_loss = loss_sum / (2.0 * total_count)
    return (hess_diag, second_moment, mean_loss)


def solution(mesh):
    placed = (
        P("dp", None),
        P("dp", None),
        P("dp"),
        P("dp", "tensor"),
        P("dp", "tensor"),
        P(),
        P("tensor"),
        P("dp", "tensor"),
    )
    return jax.shard_map(
        body,
        mesh=mesh,
        in_specs=placed,
        out_specs=(P("dp", "tensor"), P("dp", "tensor"), P()),
        check_vma=False,
    )
```

profile of v0, /device:TPU:0, one launch (start us, length us, event | category | flops | bytes accessed | tf_op | source)
XLA Modules:
  0.0 513.7 jit_solution(14408167545092987989)
XLA Ops:
  7.2 0.7 all-gather.3.cloned.1.call-update
  8.0 0.7 all-gather.5.cloned.1.call-update
  8.7 0.7 broadcast_multiply_fusion.1
  9.4 15.9 %add_convert_fusion = bf16[1792,3584]{0,1:T(8,128)(2,1)} fusion(s32[3584]{0:T(1024)} %param.14, s32[1792]{0:T(1024)S(1)} %broadcast_multiply_fusion.1), kind=kLoop, calls=%fused_computation.13 | loop fusion | flops 109182976 | bytes 12866560 | tf_op jit(solution)/shard_map/convert_element_type | solution.py:22
  25.3 142.0 %all-gather.3.cloned.1.call-done = bf16[1792,3584]{1,0:T(8,128)(2,1)} async-done(((bf16[112,3584]{1,0:T(8,128)(2,1)}), bf16[1792,3584]{1,0:T(8,128)(2,1)}) %all-gather.3.cloned.1.call-update) | async-done | bytes 12845072 | tf_op jit(solution)/shard_map/all_gather | solution.py:51
  167.3 18.2 %copy.17 = bf16[1792,3584]{0,1:T(8,128)(2,1)} copy(bf16[1792,3584]{1,0:T(8,128)(2,1)} %all-gather.3.cloned.1.call-done) | data formatting | bytes 25690112 | tf_op jit(solution)/shard_map/all_gather | solution.py:51
  185.5 15.0 %fusion.10 = f32[128,7168]{1,0:T(8,128)} fusion(bf16[128,1792]{1,0:T(8,128)(2,1)S(1)} %copy-done, bf16[1792,3584]{0,1:T(8,128)(2,1)} %add_convert_fusion, bf16[1792,3584]{0,1:T(8,128)(2,1)} %copy.17), kind=kOutput, calls=%fused_computation.14 | convolution fusion | flops 3339714560 | bytes 29818880 | tf_op jit(solution)/shard_map/dot_general | solution.py:53
  200.5 3.3 multiply_convert_fusion.1
  203.8 118.3 %all-gather.5.cloned.1.call-done = bf16[1792,3584]{1,0:T(8,128)(2,1)} async-done(((bf16[112,3584]{1,0:T(8,128)(2,1)}), bf16[1792,3584]{1,0:T(8,128)(2,1)}) %all-gather.5.cloned.1.call-update) | async-done | bytes 12845072 | tf_op jit(solution)/shard_map/all_gather | solution.py:56
  322.1 7.0 %fusion.23 = f32[256,1792]{1,0:T(8,128)S(1)} fusion(bf16[1792,3584]{1,0:T(8,128)(2,1)} %all-gather.5.cloned.1.call-done, bf16[128,3584]{1,0:T(8,128)(2,1)S(1)} %get-tuple-element.16, bf16[128,3584]{1,0:T(8,128)(2,1)S(1)} %get-tuple-element.15), kind=kOutput, calls=%fused_computation.29 | convolution fusion | flops 3292004352 | bytes 16515072 | tf_op jit(solution)/shard_map/tf,df->td/dot_general | solution.py:61
  329.1 1.4 fusion.49
  330.8 19.0 %all-reduce.4.cloned.1.call-done = (f32[128,1792]{1,0:T(8,128)}, f32[128,1792]{1,0:T(8,128)}) async-done(((f32[128,1792]{1,0:T(8,128)}, f32[128,1792]{1,0:T(8,128)}), (f32[128,1792]{1,0:T(8,128)}, f32[128,1792]{1,0:T(8,128)})) %all-reduce.4.cloned.1.call-update) | async-done | bytes 1835024 | tf_op jit(solution)/shard_map/psum | solution.py:62
  349.8 2.4 fusion.27
  352.2 6.7 %fusion.29 = f32[256,3584]{1,0:T(8,128)S(1)} fusion(bf16[1792,3584]{1,0:T(8,128)(2,1)} %all-gather.5.cloned.1.call-done, bf16[128,1792]{1,0:T(8,128)(2,1)S(1)} %get-tuple-element.21, bf16[128,1792]{1,0:T(8,128)(2,1)S(1)} %get-tuple-element.20), kind=kOutput, calls=%fused_computation.40 | convolution fusion | flops 3290169344 | bytes 17432576 | tf_op jit(solution)/shard_map/dot_general | solution.py:68
  358.9 17.8 %bitcast_multiply_fusion = f32[1792,3584]{0,1:T(8,128)} fusion(bf16[128,1792]{1,0:T(8,128)(2,1)S(1)} %copy-done, s32[3584]{0:T(1024)S(1)} %copy-done.5, s32[1792]{0:T(1024)S(1)} %broadcast_multiply_fusion.1, f32[256,3584]{1,0:T(8,128)S(1)} %fusion.29, f32[128,7168]{1,0:T(8,128)S(1)} %copy-done.2), kind=kOutput, calls=%fused_computation.12 | convolution fusion | flops 1779957760 | bytes 33510400 | tf_op jit(solution)/shard_map/tr,tf->rf/dot_general | solution.py:77
  376.8 26.7 %reshape.13 = f32[1792,256,14]{0,2,1:T(8,128)} reshape(f32[1792,3584]{0,1:T(8,128)} %bitcast_multiply_fusion) | data formatting | bytes 51380224 | tf_op jit(solution)/shard_map/reshape | solution.py:81
  403.5 13.6 %reduce_sum.27 = f32[1792,256]{0,1:T(8,128)} reduce(f32[1792,256,14]{0,2,1:T(8,128)} %reshape.13, f32[]{:T(128)} %constant.21.clone.1), dimensions={2}, to_apply=%region_2.0 | reduce | flops 5963776 | bytes 27525124 | tf_op jit(solution)/shard_map/reduce_sum | solution.py:81
  417.1 1.7 broadcast_multiply_fusion
  418.9 1.7 copy.21
  422.6 41.7 %all-reduce = (f32[]{:T(128)}, f32[]{:T(128)}) all-reduce(f32[]{:T(128)S(6)} %mul.184, f32[]{:T(128)S(6)} %mul.191), channel_id=1, replica_groups=mesh['dp'=16,'tensor'=2] {'dp','tensor'}, use_global_device_ids=true, to_apply=%region_5.0 | all-reduce | flops 2 | bytes 16 | tf_op jit(solution)/shard_map/psum | solution.py:47
  465.6 37.3 %reduce-scatter.4.cloned.1.call-done = f32[112,256]{1,0:T(8,128)} async-done(((f32[1792,256]{1,0:T(8,128)}), f32[112,256]{1,0:T(8,128)}) %reduce-scatter.4.cloned.1.call-update) | async-done | bytes 114704
  502.9 1.0 copy.22
  504.5 0.7 copy.19
  505.3 0.7 copy.20
  (24 shorter events, 1.8 us)
Async XLA Ops:
  7.2 178.3 %copy-start = (bf16[128,1792]{1,0:T(8,128)(2,1)S(1)}, bf16[128,1792]{1,0:T(8,128)(2,1)}, u32[]{:S(2)}) copy-start(bf16[128,1792]{1,0:T(8,128)(2,1)} %param.8) | copy-start | bytes 1376260
  7.2 160.1 %all-gather.3.cloned.1.call-start = ((), (), s32[]{:S(2)}) async-start(), calls=%async_computation.1 | async-start | bytes 13647872 | tf_op jit(solution)/shard_map/all_gather | solution.py:51
  7.9 314.2 %all-gather.5.cloned.1.call-start = ((), (), s32[]{:S(2)}) async-start(), calls=%async_computation.2 | async-start | bytes 13647872 | tf_op jit(solution)/shard_map/all_gather | solution.py:56
  8.7 341.1 %all-reduce.4.cloned.1.call-start = ((), (), s32[]{:S(2)}) async-start(), calls=%async_computation.4 | async-start | bytes 3670016 | tf_op jit(solution)/shard_map/psum | solution.py:62
  329.1 1.6 copy-start.6
  329.1 20.7 %copy-start.3 = (bf16[128,1792]{1,0:T(8,128)(2,1)S(1)}, bf16[128,1792]{1,0:T(8,128)(2,1)}, u32[]{:S(2)}) copy-start(bf16[128,1792]{1,0:T(8,128)(2,1)} %param.9) | copy-start | bytes 1376260
  330.5 172.3 %reduce-scatter.4.cloned.1.call-start = ((), (), s32[]{:S(2)}) async-start(), calls=%async_computation.3 | async-start | bytes 1949696
  352.2 6.7 %copy-start.2 = (f32[128,7168]{1,0:T(8,128)S(1)}, f32[128,7168]{1,0:T(8,128)}, u32[]{:S(2)}) copy-start(f32[128,7168]{1,0:T(8,128)} %fusion.10) | copy-start | bytes 11010052
  352.2 6.7 %copy-start.5 = (s32[3584]{0:T(1024)S(1)}, s32[3584]{0:T(1024)}, u32[]{:S(2)}) copy-start(s32[3584]{0:T(1024)} %param.14) | copy-start | bytes 43012
  417.1 88.9 %copy-start.1 = (bf16[128,1792]{1,0:T(8,128)(2,1)S(1)}, bf16[128,1792]{1,0:T(8,128)(2,1)}, u32[]{:S(2)}) copy-start(bf16[128,1792]{1,0:T(8,128)(2,1)} %param.8) | copy-start | bytes 1376260
  418.8 3.7 copy-start.4
Sparse Core Ops, SparseCore 0:
  10.7 156.5 all-gather.2
  170.0 152.0 all-gather.4
  330.6 19.1 all-reduce.3
  420.7 82.0 reduce-scatter.3
where the time goes:
time: 515 us; the launch traced here: 514 us
  waiting for transfers between devices  318 us (62%)
  local copies, waits for them, and re-layouts  50.6 us (10%)
  matrix products  46.6 us (9%)
  blocking collectives  41.7 us (8%)
  other arithmetic  38.9 us (8%)
  between operations  17.6 us (3%)
    all_gather x1, waiting for transfers between devices, body(): lax.all_gather(up_weight, 'dp', axis=0, tiled=True)  142 us
    all_gather x1, waiting for transfers between devices, body(): full_down = lax.all_gather(down_weight, 'dp', axis=0, tiled=True)  118 us
    psum x1, blocking collectives, body(): total_count = lax.psum(local_count, ('dp', 'tensor'))  41.7 us
    unnamed x5, waiting for transfers between devices  38.7 us
    reshape x1, local copies, waits for them, and re-layouts, body(): hutch_terms.reshape(own_rows * lax.axis_size('dp'), ff_local // BLOCK, BL...  26.7 us
    psum x1, waiting for transfers between devices, body(): lax.psum((projected[:tok_count], projected[tok_count:]), 'tensor')  19 us
    all_gather x1, local copies, waits for them, and re-layouts, body(): lax.all_gather(up_weight, 'dp', axis=0, tiled=True)  18.2 us
    dot_general x1, matrix products, body(): jnp.einsum('tr,tf->rf', columns, chain_grad, preferred_element_type=jnp.f...  17.8 us
  transfers between devices with their start and end apart: 4, of which 4 were waited for; matrix products, arithmetic and copies ran while one was open for 10% of the time, Pallas kernels for 0%

commit v1 on v0

v1 whole, which is shorter than its diff:
```python
import math
import jax
import jax.numpy as jnp
from jax import lax
from jax.sharding import Mesh, PartitionSpec as P

BLOCK = 14
FFX, TKX = "hi", "lo"

gelu_coef = 0.7978845608028654
cubic_coef = 0.044715
beta_two = 0.999


def probe_signs(row_keys, col_keys):
    hashed = jnp.bitwise_xor(row_keys[:, None] * 747796405, col_keys[None, :])
    hashed = jnp.bitwise_xor(hashed, jnp.right_shift(hashed, 15) & 131071)
    hashed = hashed * 695872825
    hashed = jnp.bitwise_xor(hashed, jnp.right_shift(hashed, 13) & 524287)
    hashed = hashed * 739982445
    hashed = jnp.bitwise_xor(hashed, jnp.right_shift(hashed, 16) & 65535)
    parity = jnp.right_shift(hashed, 11) & 1
    return (2 * parity - 1).astype(jnp.bfloat16)


def gelu_parts(preact):
    tanh_arg = gelu_coef * (preact + cubic_coef * preact * preact * preact)
    tanh_val = jnp.tanh(tanh_arg)
    sech_sq = 1.0 - tanh_val * tanh_val
    arg_slope = gelu_coef * (1.0 + 3.0 * cubic_coef * preact * preact)
    arg_curve = gelu_coef * 6.0 * cubic_coef * preact
    gelu_value = 0.5 * preact * (1.0 + tanh_val)
    gelu_slope = 0.5 * (1.0 + tanh_val) + 0.5 * preact * sech_sq * arg_slope
    gelu_curve = sech_sq * (
        arg_slope - preact * tanh_val * arg_slope * arg_slope + 0.5 * preact * arg_curve
    )
    return (gelu_value, gelu_slope, gelu_curve)


def spread(weight):
    own_rows, ff_held = weight.shape
    groups = lax.axis_size(FFX)
    cols = ff_held // groups
    pieces = lax.all_to_all(weight.reshape(own_rows, groups, cols), FFX, split_axis=1, concat_axis=0)
    full = lax.all_gather(pieces, TKX, axis=1 if FFX == "hi" else 0)
    return full.reshape(-1, cols)


def body(tokens, targets, live_mask, up_weight, down_weight, probe_rows, probe_cols, moment):
    tok_count, features = tokens.shape
    own_rows, ff_held = up_weight.shape
    groups = lax.axis_size(FFX)
    cols = ff_held // groups
    cores = lax.axis_size("tensor")
    everyone = ("hi", "lo", "tensor")
    share = tok_count // cores
    col_keys = lax.dynamic_slice_in_dim(probe_cols, lax.axis_index(FFX) * cols, cols)
    signs = probe_signs(probe_rows, col_keys)
    first = lax.axis_index("tensor") * share
    live_own = lax.dynamic_slice_in_dim(live_mask, first, share).astype(jnp.float32)
    targets_own = lax.dynamic_slice_in_dim(targets, first, share)
    all_tokens = lax.all_gather(tokens, FFX, axis=0, tiled=True)
    up_full = spread(up_weight)
    down_full = spread(down_weight)
    preact = jnp.dot(all_tokens, up_full, preferred_element_type=jnp.float32)
    tangent = jnp.dot(all_tokens, signs, preferred_element_type=jnp.float32)
    gelu_value, gelu_slope, gelu_curve = gelu_parts(preact)
    hidden = gelu_value.astype(jnp.bfloat16)
    hidden_dir = (gelu_slope * tangent).astype(jnp.bfloat16)
    stacked = jnp.stack([hidden, hidden_dir])
    projected = jnp.einsum("ntf,df->ntd", stacked, down_full, preferred_element_type=jnp.float32)
    part = projected.astype(jnp.bfloat16).reshape(2, groups * cores, share, features)
    part = lax.all_to_all(part, (FFX, "tensor"), split_axis=1, concat_axis=0)
    outputs, out_dir = jnp.sum(part.astype(jnp.float32), axis=0)
    diff = outputs - targets_own.astype(jnp.float32)
    weighted = live_own[:, None] * diff
    residual = jnp.stack([weighted, live_own[:, None] * out_dir]).astype(jnp.bfloat16)
    residual = lax.all_gather(residual, (FFX, "tensor"), axis=1, tiled=True)
    sums = lax.psum(jnp.stack([jnp.sum(weighted * diff), jnp.sum(live_own)]), everyone)
    loss_sum, total_count = sums[0], sums[1]
    grads = jnp.einsum("ntd,df->ntf", residual, down_full, preferred_element_type=jnp.float32)
    chain_grad = (grads[1] * gelu_slope + grads[0] * gelu_curve * tangent).astype(jnp.bfloat16)
    product = jnp.einsum("tr,tf->rf", all_tokens, chain_grad, preferred_element_type=jnp.float32)
    blocks = cols // BLOCK
    member = (
        lax.broadcasted_iota(jnp.int32, (cols, blocks), 0) // BLOCK
        == lax.broadcasted_iota(jnp.int32, (cols, blocks), 1)
    ).astype(jnp.float32)
    summed = jnp.dot(signs.astype(jnp.float32) * product, member, precision=lax.Precision.HIGH)
    summed = summed.reshape(lax.axis_size("hi"), lax.axis_size("lo"), own_rows, blocks)
    tk_dim = 1 if TKX == "lo" else 0
    summed = lax.all_to_all(summed, TKX, split_axis=tk_dim, concat_axis=0).sum(axis=0)
    summed = lax.all_to_all(summed, FFX, split_axis=0, concat_axis=1).reshape(own_rows, groups * blocks)
    hess_diag = summed * (1.0 / BLOCK) / total_count
    second_moment = beta_two * moment + (1.0 - beta_two) * hess_diag * hess_diag
    mean_loss = loss_sum / (2.0 * total_count)
    return (hess_diag, second_moment, mean_loss)


def solution(mesh):
    dp = mesh.shape["dp"]
    hi = math.gcd(dp, 4)
    split = Mesh(mesh.devices.reshape(hi, dp // hi, mesh.shape["tensor"]), ("hi", "lo", "tensor"))
    rows = ("hi", "lo")
    placed = (
        P(rows, None),
        P(rows, None),
        P(rows),
        P(rows, "tensor"),
        P(rows, "tensor"),
        P(),
        P("tensor"),
        P(rows, "tensor"),
    )
    return jax.shard_map(
        body,
        mesh=split,
        in_specs=placed,
        out_specs=(P(rows, "tensor"), P(rows, "tensor"), P()),
        check_vma=False,
    )
```

time: 515 us -> 397 us (0.77)
  waiting for transfers between devices: 318 us -> 196 us
  blocking collectives: 41.7 us -> 125 us
  local copies, waits for them, and re-layouts: 50.6 us -> 14.8 us
  other arithmetic: 38.9 us -> 9.84 us
  matrix products: 46.6 us -> 25.3 us
  starting transfers between devices: 0.34 us -> 8.39 us
    all_gather x2 -> x4, waiting for transfers between devices: 260 us -> 113 us  [the longest x2 72.7 us: spread(): full = lax.all_gather(pieces, TKX, axis=1 if FFX == 'hi' else 0)]
    all_to_all x0 -> x3, blocking collectives: none -> 85.4 us  [the longest x2 73 us: spread(): lax.all_to_all(weight.reshape(own_rows, groups, cols), FFX, split_axis=1,...]
    all_to_all x0 -> x2, waiting for transfers between devices: none -> 81.9 us  [the longest x1 81.9 us: body(): part = lax.all_to_all(part, (FFX, 'tensor'), split_axis=1, concat_axis=0)]
    unnamed x5 -> x4, waiting for transfers between devices: 38.7 us -> 0.73 us
    reshape x1 -> x0, local copies, waits for them, and re-layouts: 26.7 us -> none  [body(): hutch_terms.reshape(own_rows * lax.axis_size('dp'), ff_local // BLOCK, BL...]
    dot_general x4 -> x6, matrix products: 46.6 us -> 25.3 us  [the longest x1 6.14 us: body(): jnp.einsum('ntd,df->ntf', residual, down_full, preferred_element_type=jnp...]
    convert_element_type x3 -> x0, other arithmetic: 19.2 us -> none  [the longest x1 15.9 us: probe_signs(): return (2 * parity - 1).astype(jnp.bfloat16)]
    psum x1 -> x0, waiting for transfers between devices: 19 us -> none  [body(): lax.psum((projected[:tok_count], projected[tok_count:]), 'tensor')]
  transfers between devices with their start and end apart: 4 -> 6, of which waited for: 4 -> 4; matrix products, arithmetic and copies ran while one was open for 10% -> 4% of each run, Pallas kernels for 0% -> 0%
where the time goes in v1:
time: 397 us; the launch traced here: 396 us
  waiting for transfers between devices  196 us (49%)
  blocking collectives  125 us (31%)
  matrix products  25.3 us (6%)
  between operations  16.5 us (4%)
  local copies, waits for them, and re-layouts  14.8 us (4%)
  other arithmetic  9.84 us (2%)
  starting transfers between devices  8.39 us (2%)
    all_to_all x1, waiting for transfers between devices, body(): part = lax.all_to_all(part, (FFX, 'tensor'), split_axis=1, concat_axis=0)  81.9 us
    all_to_all x2, blocking collectives, spread(): lax.all_to_all(weight.reshape(own_rows, groups, cols), FFX, split_axis=1,...  73 us
    all_gather x2, waiting for transfers between devices, spread(): full = lax.all_gather(pieces, TKX, axis=1 if FFX == 'hi' else 0)  72.7 us
    all_gather x1, waiting for transfers between devices, body(): residual = lax.all_gather(residual, (FFX, 'tensor'), axis=1, tiled=True)  40.6 us
    psum x1, blocking collectives, body(): lax.psum(jnp.stack([jnp.sum(weighted * diff), jnp.sum(live_own)]), everyone)  39.8 us
    all_to_all x1, blocking collectives, body(): lax.all_to_all(summed, TKX, split_axis=tk_dim, concat_axis=0).sum(axis=0)  12.4 us
  transfers between devices with their start and end apart: 6, of which 4 were waited for; matrix products, arithmetic and copies ran while one was open for 4% of the time, Pallas kernels for 0%

profile of v1, /device:TPU:0, one launch (start us, length us, event | category | flops | bytes accessed | tf_op | source)
XLA Modules:
  0.0 396.0 jit_solution(3567373051237911727)
XLA Ops:
  8.0 1.8 broadcast_in_dim_reshape.12
  9.9 45.5 %all_to_all.57 = bf16[1,112,4,896]{3,1,0,2:T(8,128)(2,1)} all-to-all(bf16[1,112,4,896]{3,1,0,2:T(8,128)(2,1)S(1)} %copy.49), channel_id=1, replica_groups=mesh['hi'=4,'lo'=4,'tensor'=2] {'hi'}, dimensions={2} | all-to-all | bytes 1605632 | tf_op jit(solution)/shard_map/all_to_all | solution.py:44
  55.7 27.6 %all_to_all.58 = bf16[1,112,4,896]{3,1,0,2:T(8,128)(2,1)} all-to-all(bf16[1,112,4,896]{3,1,0,2:T(8,128)(2,1)S(1)} %copy.53), channel_id=1, replica_groups=mesh['hi'=4,'lo'=4,'tensor'=2] {'hi'}, dimensions={2} | all-to-all | bytes 1605632 | tf_op jit(solution)/shard_map/all_to_all | solution.py:44
  84.1 5.1 %fusion.8 = f32[896,512]{0,1:T(8,128)S(1)} fusion(bf16[512,1792]{1,0:T(8,128)(2,1)} %all-gather.7.cloned.1.call-done, s32[896]{0:T(1024)S(1)} %dynamic_slice.9, s32[1792]{0:T(1024)S(1)} %broadcast_multiply_fusion), kind=kOutput, calls=%fused_computation.14 | convolution fusion | flops 1671462912 | bytes 3680768 | tf_op jit(solution)/shard_map/dot_general | solution.py:66
  89.2 34.8 %all-gather.11.cloned.1.call-done = bf16[4,4,112,1,896]{4,2,3,0,1:T(8,128)(2,1)} async-done(((bf16[4,1,112,1,896]{4,2,3,0,1:T(8,128)(2,1)}), bf16[4,4,112,1,896]{4,2,3,0,1:T(8,128)(2,1)}) %all-gather.11.cloned.1.call-update) | async-done | bytes 3211280 | tf_op jit(solution)/shard_map/all_gather | solution.py:45
  124.0 2.3 copy.51
  126.4 2.1 fusion.72
  128.5 1.3 copy-done.2
  129.8 2.6 fusion.24
  132.3 37.9 %all-gather.13.cloned.1.call-done = bf16[4,4,112,1,896]{4,2,3,0,1:T(8,128)(2,1)} async-done(((bf16[4,1,112,1,896]{4,2,3,0,1:T(8,128)(2,1)}), bf16[4,4,112,1,896]{4,2,3,0,1:T(8,128)(2,1)}) %all-gather.13.cloned.1.call-update) | async-done | bytes 3211280 | tf_op jit(solution)/shard_map/all_gather | solution.py:45
  170.3 2.3 copy.55
  172.7 4.3 %convolution_convert_fusion = bf16[2,512,1792]{2,1,0:T(8,128)(2,1)S(1)} fusion(bf16[1792,896,1]{1,0,2:T(8,128)(2,1)S(1)} %bitcast.75, bf16[1,512,896]{2,1,0:T(8,128)(2,1)S(1)} %copy-done.5, bf16[1,512,896]{2,1,0:T(8,128)(2,1)S(1)} %copy-done.4), kind=kOutput, calls=%fused_computation.13 | convolution fusion | flops 3291086848 | bytes 8716288 | tf_op jit(solution)/shard_map/ntf,df->ntd/dot_general | solution.py:71
  176.9 2.1 copy.56
  179.0 4.7 %all-to-all-start.2 = ((bf16[1,2,8,64,1792]{4,3,1,0,2:T(8,128)(2,1)}), bf16[1,2,8,64,1792]{4,3,1,0,2:T(8,128)(2,1)}, u32[]{:S(2)}, u32[]{:S(2)}) async-start(bf16[1,2,8,64,1792]{4,3,1,0,2:T(8,128)(2,1)} %copy.56), calls=%async_computation.2 | async-start | bytes 7340032 | tf_op jit(solution)/shard_map/all_to_all | solution.py:73
  184.7 81.9 %all-to-all-done.2 = bf16[1,2,8,64,1792]{4,3,1,0,2:T(8,128)(2,1)} async-done(((bf16[1,2,8,64,1792]{4,3,1,0,2:T(8,128)(2,1)}), bf16[1,2,8,64,1792]{4,3,1,0,2:T(8,128)(2,1)}, u32[]{:S(2)}, u32[]{:S(2)}) %all-to-all-start.2) | async-done | bytes 3670048 | tf_op jit(solution)/shard_map/all_to_all | solution.py:73
  266.6 2.7 convert_reduce_fusion
  271.1 40.6 %all-gather.9.cloned.1.call-done = bf16[2,512,1792]{2,1,0:T(8,128)(2,1)} async-done(((bf16[2,64,1792]{2,1,0:T(8,128)(2,1)}), bf16[2,512,1792]{2,1,0:T(8,128)(2,1)}) %all-gather.9.cloned.1.call-update) | async-done | bytes 3670032 | tf_op jit(solution)/shard_map/all_gather | solution.py:78
  311.7 6.1 %fusion.73 = f32[2,512,896]{2,1,0:T(8,128)S(1)} fusion(bf16[2,512,1792]{2,1,0:T(8,128)(2,1)} %all-gather.9.cloned.1.call-done, bf16[1792,896,1]{1,0,2:T(8,128)(2,1)S(1)} %bitcast.76), kind=kOutput, calls=%fused_computation.102 | convolution fusion | flops 3288334336 | bytes 10551296 | tf_op jit(solution)/shard_map/ntd,df->ntf/dot_general | solution.py:81
  317.9 3.4 fusion.25
  321.3 4.4 %fusion.6 = f32[1792,64]{0,1:T(8,128)S(1)} fusion(f32[896,1792]{1,0:T(8,128)S(1)} %fusion.25, s32[896]{0:T(1024)S(1)} %dynamic_slice.9, s32[1792]{0:T(1024)S(1)} %broadcast_multiply_fusion, s32[896]{0:T(1024)S(1)} %get-tuple-element.26, s32[896]{0:T(1024)S(1)} %get-tuple-element.27, pred[896]{0:T(1024)(128)(4,1)S(1)} %fusion.38), kind=kOutput, calls=%fused_computation.10 | convolution fusion | flops 647184384 | bytes 6900096 | tf_op jit(solution)/shard_map/dot_general | solution.py:89
  326.5 12.4 %all_to_all.59 = f32[1,4,4,112,64]{3,1,4,0,2:T(4,128)S(1)} all-to-all(f32[1,4,4,112,64]{3,1,4,0,2:T(4,128)S(1)} %copy.57), channel_id=1, replica_groups=mesh['hi'=4,'lo'=4,'tensor'=2] {'lo'}, dimensions={2} | all-to-all | bytes 917504 | tf_op jit(solution)/shard_map/all_to_all | solution.py:92
  339.7 3.3 all-to-all-start.4
  343.0 1.4 pad_maximum_fusion.1
  344.5 39.8 %psum.7 = f32[2]{0:T(128)S(1)} all-reduce(f32[2]{0:T(128)S(1)} %pad_maximum_fusion.1), channel_id=1, replica_groups=mesh['hi'=4,'lo'=4,'tensor'=2] {'hi','lo','tensor'}, use_global_device_ids=true, to_apply=%region_4.5 | all-reduce | flops 2 | bytes 16 | tf_op jit(solution)/shard_map/psum | solution.py:79
  (56 shorter events, 9.3 us)
Async XLA Ops:
  7.2 48.3 %copy-start.6 = (bf16[112,3584]{1,0:T(8,128)(2,1)S(1)}, bf16[112,3584]{1,0:T(8,128)(2,1)}, u32[]{:S(2)}) copy-start(bf16[112,3584]{1,0:T(8,128)(2,1)} %param.12) | copy-start | bytes 2408452
  7.2 76.9 %all-gather.7.cloned.1.call-start = ((), (), s32[]{:S(2)}) async-start(), calls=%async_computation.5 | async-start | bytes 2293760 | tf_op jit(solution)/shard_map/all_gather | solution.py:62
  7.9 116.1 %all-gather.11.cloned.1.call-start = ((), (), s32[]{:S(2)}) async-start(), calls=%async_computation.7 | async-start | bytes 4014080 | tf_op jit(solution)/shard_map/all_gather | solution.py:45
  55.4 28.7 %copy-start.9 = (s32[1792]{0:T(1024)S(1)}, s32[1792]{0:T(1024)}, u32[]{:S(2)}) copy-start(s32[1792]{0:T(1024)} %param.13) | copy-start | bytes 21508
  55.4 114.8 %all-gather.13.cloned.1.call-start = ((), (), s32[]{:S(2)}) async-start(), calls=%async_computation.8 | async-start | bytes 4014080 | tf_op jit(solution)/shard_map/all_gather | solution.py:45
  89.2 39.3 %copy-start = (f32[896,512]{0,1:T(8,128)}, f32[896,512]{0,1:T(8,128)S(1)}, u32[]{:S(2)}) copy-start(f32[896,512]{0,1:T(8,128)S(1)} %fusion.8) | copy-start | bytes 5505028
  124.0 2.5 copy-start.11
  128.5 1.3 copy-start.2
  170.2 2.3 copy-start.4
  170.2 2.4 copy-start.5
  179.0 5.0 %copy-start.10 = (s32[128]{0:T(128)S(1)}, s32[128]{0:T(128)}, u32[]{:S(2)}) copy-start(s32[128]{0:T(128)} %param.10) | copy-start | bytes 1540
  179.0 87.6 %all-to-all-start.2 = ((bf16[1,2,8,64,1792]{4,3,1,0,2:T(8,128)(2,1)}), bf16[1,2,8,64,1792]{4,3,1,0,2:T(8,128)(2,1)}, u32[]{:S(2)}, u32[]{:S(2)}) async-start(bf16[1,2,8,64,1792]{4,3,1,0,2:T(8,128)(2,1)} %copy.56), calls=%async_computation.2 | async-start | bytes 7340032 | tf_op jit(solution)/shard_map/all_to_all | solution.py:73
  183.8 127.9 %all-gather.9.cloned.1.call-start = ((), (), s32[]{:S(2)}) async-start(), calls=%async_computation.6 | async-start | bytes 4128768 | tf_op jit(solution)/shard_map/all_gather | solution.py:78
  266.6 2.8 copy-start.8
  311.7 6.2 %copy-start.1 = (f32[896,512]{0,1:T(8,128)S(1)}, f32[896,512]{0,1:T(8,128)}, u32[]{:S(2)}) copy-start(f32[896,512]{0,1:T(8,128)} %copy-done) | copy-start | bytes 5505028
  311.7 6.2 %copy-start.3 = (f32[512,896]{1,0:T(8,128)S(1)}, f32[512,896]{1,0:T(8,128)}, u32[]{:S(2)}) copy-start(f32[512,896]{1,0:T(8,128)} %copy-done.2) | copy-start | bytes 5505028
  311.7 6.2 %copy-start.12 = (bf16[512,1792]{1,0:T(8,128)(2,1)S(1)}, bf16[512,1792]{1,0:T(8,128)(2,1)}, u32[]{:S(2)}) copy-start(bf16[512,1792]{1,0:T(8,128)(2,1)} %all-gather.7.cloned.1.call-done) | copy-start | bytes 5505028
  325.7 18.7 %copy-start.7 = (f32[112,256]{1,0:T(8,128)S(1)}, f32[112,256]{1,0:T(8,128)}, u32[]{:S(2)}) copy-start(f32[112,256]{1,0:T(8,128)} %param.15) | copy-start | bytes 344068
  339.7 46.4 %all-to-all-start.4 = ((f32[4,112,1,64]{1,3,2,0:T(8,128)}), f32[4,112,1,64]{1,3,2,0:T(8,128)S(1)}, u32[]{:S(2)}, u32[]{:S(2)}) async-start(f32[4,112,1,64]{1,3,2,0:T(8,128)} %copy.59), calls=%async_computation.4 | async-start | bytes 262144 | tf_op jit(solution)/shard_map/all_to_all | solution.py:93
Sparse Core Ops, SparseCore 0:
  9.5 69.6 all-gather.6
  81.1 42.8 all-gather.10
  125.8 44.3 all-gather.12
  271.2 40.4 all-gather.8

commit v2 on v1

v2 whole, which is shorter than its diff:
```python
import functools
import math
import jax
import jax.numpy as jnp
from jax import lax
from jax.experimental import pallas as pl
from jax.experimental.pallas import tpu as pltpu
from jax.sharding import Mesh, PartitionSpec as P

BLOCK = 14

gelu_coef = 0.7978845608028654
cubic_coef = 0.044715
beta_two = 0.999


def probe_signs(row_keys, col_keys):
    hashed = jnp.bitwise_xor(row_keys[:, None] * 747796405, col_keys[None, :])
    hashed = jnp.bitwise_xor(hashed, jnp.right_shift(hashed, 15) & 131071)
    hashed = hashed * 695872825
    hashed = jnp.bitwise_xor(hashed, jnp.right_shift(hashed, 13) & 524287)
    hashed = hashed * 739982445
    hashed = jnp.bitwise_xor(hashed, jnp.right_shift(hashed, 16) & 65535)
    parity = jnp.right_shift(hashed, 11) & 1
    return (2 * parity - 1).astype(jnp.bfloat16)


def gelu_parts(preact):
    tanh_arg = gelu_coef * (preact + cubic_coef * preact * preact * preact)
    tanh_val = jnp.tanh(tanh_arg)
    sech_sq = 1.0 - tanh_val * tanh_val
    arg_slope = gelu_coef * (1.0 + 3.0 * cubic_coef * preact * preact)
    arg_curve = gelu_coef * 6.0 * cubic_coef * preact
    gelu_value = 0.5 * preact * (1.0 + tanh_val)
    gelu_slope = 0.5 * (1.0 + tanh_val) + 0.5 * preact * sech_sq * arg_slope
    gelu_curve = sech_sq * (
        arg_slope - preact * tanh_val * arg_slope * arg_slope + 0.5 * preact * arg_curve
    )
    return (gelu_value, gelu_slope, gelu_curve)


MESH = pl.DeviceIdType.MESH
ANY = pl.BlockSpec(memory_space=pl.ANY)
VMEM = pl.BlockSpec(memory_space=pltpu.VMEM)


def remote(src, dst, send_sem, recv_sem, device):
    return pltpu.make_async_remote_copy(
        src_ref=src, dst_ref=dst, send_sem=send_sem, recv_sem=recv_sem, device_id=device, device_id_type=MESH
    )


def gather_kernel(
    n, groups, tok_ref, up_ref, down_ref, tok_all, up_all, down_all,
    own_sem, tok_send, tok_recv, swap_send, swap_recv, line_send, line_recv,
):
    z, g, c = lax.axis_index("hi"), lax.axis_index("lo"), lax.axis_index("tensor")
    cols = up_all.shape[3]
    barrier = pltpu.get_barrier_semaphore()
    for d in range(1, groups):
        pl.semaphore_signal(barrier, inc=1, device_id=(z, lax.rem(g + d, groups), c), device_id_type=MESH)

    for side in (1, n - 1):
        pl.semaphore_signal(barrier, inc=1, device_id=(lax.rem(z + side, n), g, c), device_id_type=MESH)
    pl.semaphore_wait(barrier, groups + 1)

    def cut(ref, at):
        return ref.at[:, pl.ds(pl.multiple_of(at * cols, cols), cols)]

    held = ((up_ref, up_all), (down_ref, down_all))

    def swap(w, d):
        to = lax.rem(g + d, groups)
        return remote(cut(held[w][0], to), held[w][1].at[z, g], swap_send.at[w, d - 1], swap_recv.at[w, d - 1], (z, to, c))

    def swapped(w, d):
        came = lax.rem(g + groups - d, groups)
        return remote(cut(held[w][0], came), held[w][1].at[z, came], swap_send.at[w, d - 1], swap_recv.at[w, d - 1], (z, came, c))

    def token_send(d):
        to = lax.rem(g + d, groups)
        return remote(tok_ref, tok_all.at[g], tok_send.at[d - 1], tok_recv.at[d - 1], (z, to, c))

    def token_got(d):
        came = lax.rem(g + groups - d, groups)
        return remote(tok_ref, tok_all.at[came], tok_send.at[d - 1], tok_recv.at[d - 1], (z, came, c))

    def hop(w, way, d, s):
        step = 1 if way == 0 else -1
        slot = held[w][1].at[z - step * s, lax.rem(g + groups - d, groups)]
        return remote(slot, slot, line_send.at[w, way, d, s], line_recv.at[w, way, d, s], (z + step, g, c))

    def arrival(w, way, d, s):
        step = 1 if way == 0 else -1
        slot = held[w][1].at[z - step * s, lax.rem(g + groups - d, groups)]
        return remote(slot, slot, line_send.at[w, way, d, s - 1], line_recv.at[w, way, d, s - 1], (z - step, g, c))

    def goes(way, s):
        if way == 0:
            return (z < n - 1) & (z - s >= 0)
        return (z > 0) & (z + s <= n - 1)

    def comes(way, s):
        return z - s >= 0 if way == 0 else z + s <= n - 1

    owns = [pltpu.make_async_copy(cut(src, g), dst.at[z, g], own_sem.at[w]) for w, (src, dst) in enumerate(held)]
    owns.append(pltpu.make_async_copy(tok_ref, tok_all.at[g], own_sem.at[2]))
    for copy in owns:
        copy.start()
    for d in range(1, groups):
        swap(0, d).start()
    for d in range(1, groups):
        token_send(d).start()
    for d in range(1, groups):
        swap(1, d).start()
    for w in range(2):
        for d in range(groups):
            if d == 0:
                owns[w].wait()
            else:
                swapped(w, d).wait_recv()
            for way in range(2):
                @pl.when(goes(way, 0))
                def _():
                    hop(w, way, d, 0).start()

        @pl.loop(1, n)
        def _(s):
            for d in range(groups):
                for way in range(2):
                    @pl.when(comes(way, s))
                    def _():
                        arrival(w, way, d, s).wait_recv()

                    @pl.when(goes(way, s))
                    def _():
                        hop(w, way, d, s).start()

    owns[2].wait()
    for d in range(1, groups):
        token_send(d).wait_send()
        token_got(d).wait_recv()
    for w in range(2):
        for d in range(1, groups):
            swap(w, d).wait_send()

        @pl.loop(0, n - 1)
        def _(s):
            for d in range(groups):
                for way in range(2):
                    @pl.when(goes(way, s))
                    def _():
                        hop(w, way, d, s).wait_send()


def gather(n, groups, tokens, up_weight, down_weight):
    tok_count, features = tokens.shape
    own_rows, ff_held = up_weight.shape
    full = jax.ShapeDtypeStruct((n, groups, own_rows, ff_held // groups), up_weight.dtype)
    dma = pltpu.SemaphoreType.DMA
    return pl.pallas_call(
        functools.partial(gather_kernel, n, groups),
        name="gather",
        out_shape=(jax.ShapeDtypeStruct((groups, tok_count, features), tokens.dtype), full, full),
        in_specs=[ANY] * 3,
        out_specs=(ANY,) * 3,
        scratch_shapes=[
            dma((3,)), dma((groups - 1,)), dma((groups - 1,)), dma((2, groups - 1)), dma((2, groups - 1)),
            dma((2, 2, groups, n - 1)), dma((2, 2, groups, n - 1)),
        ],
        compiler_params=pltpu.CompilerParams(collective_id=0, has_side_effects=True),
    )(tokens, up_weight, down_weight)


def residual_kernel(
    groups, cores, out_ref, dir_ref, targets_ref, live_ref, res_all, tile_all,
    half_out, half_dir, send_out, send_dir, got_out, got_dir,
    half_send, half_recv, part_send, part_recv, res_send, res_recv, pass_send, pass_recv, tile_send, tile_recv,
):
    z, g, c = lax.axis_index("hi"), lax.axis_index("lo"), lax.axis_index("tensor")
    twin = 1 - c
    barrier = pltpu.get_barrier_semaphore()
    others = [(d, e) for d in range(groups) for e in range(cores) if (d, e) != (0, 0)]

    def at(d, e):
        return (z, lax.rem(g + d, groups), lax.rem(c + e, cores))

    def back(d, e):
        return (z, lax.rem(g + groups - d, groups), lax.rem(c + cores - e, cores))

    for d, e in others:
        pl.semaphore_signal(barrier, inc=1, device_id=at(d, e), device_id_type=MESH)
    pl.semaphore_wait(barrier, len(others))

    def halves(d):
        to = lax.rem(g + d, groups)
        return (
            remote(out_ref.at[to, twin], half_out.at[d], half_send.at[0, d], half_recv.at[0, d], (z, g, twin)),
            remote(dir_ref.at[to, twin], half_dir.at[d], half_send.at[1, d], half_recv.at[1, d], (z, g, twin)),
        )

    def parts(d):
        return (
            remote(send_out.at[d], got_out.at[d - 1], part_send.at[0, d - 1], part_recv.at[0, d - 1], at(d, 0)),
            remote(send_dir.at[d], got_dir.at[d - 1], part_send.at[1, d - 1], part_recv.at[1, d - 1], at(d, 0)),
        )

    order = list(range(1, groups)) + [0]
    for d in order:
        for copy in halves(d):
            copy.start()
    for d in order:
        to = lax.rem(g + d, groups)
        for copy in halves(d):
            copy.wait_recv()
        total = out_ref[to, c].astype(jnp.float32) + half_out[d].astype(jnp.float32)
        send_out[d] = total.astype(jnp.bfloat16)
        send_dir[d] = dir_ref[to, c] + half_dir[d]
        if d:
            for copy in parts(d):
                copy.start()
    outputs = total
    out_dir = send_dir[0]
    for d in range(1, groups):
        for copy in parts(d):
            copy.wait_recv()
        outputs += got_out[d - 1].astype(jnp.float32)
        out_dir += got_dir[d - 1]
    live = live_ref[...]
    diff = outputs - targets_ref[...].astype(jnp.float32)
    weighted = live * diff
    res_all[0, g, c] = weighted.astype(jnp.bfloat16)
    res_all[1, g, c] = (live * out_dir).astype(jnp.bfloat16)
    loss = jnp.sum(weighted * diff, keepdims=True)
    count = jnp.sum(live, keepdims=True)
    tile_all[g, c] = jnp.where(lax.broadcasted_iota(jnp.int32, tile_all.shape[2:], 0) == 0, loss, count)

    def sent(d):
        slot = res_all.at[:, g, c]
        return remote(slot, slot, res_send.at[d], res_recv.at[d], at(d, 0) if d else (z, g, twin))

    def received(d):
        slot = res_all.at[:, lax.rem(g + groups - d, groups), c] if d else res_all.at[:, g, twin]
        return remote(slot, slot, res_send.at[d], res_recv.at[d], back(d, 0) if d else (z, g, twin))

    def passed(d, core):
        slot = res_all.at[:, lax.rem(g + groups - d, groups), core]
        return remote(slot, slot, pass_send.at[d - 1], pass_recv.at[d - 1], (z, g, twin))

    def tile(i, core_from, place):
        slot = tile_all.at[core_from[1], core_from[2]]
        return remote(slot, slot, tile_send.at[i], tile_recv.at[i], place)

    for d in order:
        sent(d).start()
    for i, (d, e) in enumerate(others):
        tile(i, (z, g, c), at(d, e)).start()
    for d in range(1, groups):
        received(d).wait_recv()
        passed(d, c).start()
    received(0).wait_recv()
    for i, (d, e) in enumerate(others):
        tile(i, back(d, e), back(d, e)).wait_recv()
    for d in range(1, groups):
        passed(d, twin).wait_recv()
    for d in range(groups):
        for copy in halves(d):
            copy.wait_send()
        sent(d).wait_send()
        if d:
            for copy in parts(d):
                copy.wait_send()
            passed(d, c).wait_send()
    for i, (d, e) in enumerate(others):
        tile(i, (z, g, c), at(d, e)).wait_send()


def exchange(groups, cores, out_part, dir_part, targets, live):
    share, features = targets.shape
    dma = pltpu.SemaphoreType.DMA
    bf, f32 = jnp.bfloat16, jnp.float32
    return pl.pallas_call(
        functools.partial(residual_kernel, groups, cores),
        name="residual",
        out_shape=(
            jax.ShapeDtypeStruct((2, groups, cores, share, features), bf),
            jax.ShapeDtypeStruct((groups, cores, 8, 128), f32),
        ),
        in_specs=[VMEM] * 4,
        out_specs=(VMEM,) * 2,
        scratch_shapes=[
            pltpu.VMEM((groups, share, features), bf), pltpu.VMEM((groups, share, features), f32),
            pltpu.VMEM((groups, share, features), bf), pltpu.VMEM((groups, share, features), f32),
            pltpu.VMEM((groups - 1, share, features), bf), pltpu.VMEM((groups - 1, share, features), f32),
            dma((2, groups)), dma((2, groups)), dma((2, groups - 1)), dma((2, groups - 1)),
            dma((groups,)), dma((groups,)), dma((groups - 1,)), dma((groups - 1,)),
            dma((groups * cores - 1,)), dma((groups * cores - 1,)),
        ],
        compiler_params=pltpu.CompilerParams(collective_id=1, has_side_effects=True),
    )(out_part, dir_part, targets, live)


def reduce_kernel(
    n, groups, part_ref, tile_ref, out_ref, sums_ref, got, got_tile, total,
    line_send, line_recv, tile_send, tile_recv, swap_send, swap_recv,
):
    z, g, c = lax.axis_index("hi"), lax.axis_index("lo"), lax.axis_index("tensor")
    barrier = pltpu.get_barrier_semaphore()
    for d in range(1, groups):
        pl.semaphore_signal(barrier, inc=1, device_id=(z, lax.rem(g + d, groups), c), device_id_type=MESH)
    for s in range(1, n):
        pl.semaphore_signal(barrier, inc=1, device_id=(lax.rem(z + s, n), g, c), device_id_type=MESH)
    pl.semaphore_wait(barrier, groups + n - 2)

    def line(s):
        to = lax.rem(z + s, n)
        return (
            remote(part_ref.at[to], got.at[s - 1], line_send.at[s - 1], line_recv.at[s - 1], (to, g, c)),
            remote(tile_ref, got_tile.at[s - 1], tile_send.at[s - 1], tile_recv.at[s - 1], (to, g, c)),
        )

    def swap(d):
        to = lax.rem(g + d, groups)
        return remote(total.at[to], out_ref.at[g], swap_send.at[d - 1], swap_recv.at[d - 1], (z, to, c))

    def swapped(d):
        came = lax.rem(g + groups - d, groups)
        return remote(total.at[came], out_ref.at[came], swap_send.at[d - 1], swap_recv.at[d - 1], (z, came, c))

    for s in range(1, n):
        for copy in line(s):
            copy.start()
    acc = part_ref[z]
    sums = tile_ref[...]
    for s in range(1, n):
        for copy in line(s):
            copy.wait_recv()
        acc += got[s - 1]
        sums += got_tile[s - 1]
    total[...] = acc
    sums_ref[...] = sums
    for d in range(1, groups):
        swap(d).start()
    out_ref[g] = total[g]
    for d in range(1, groups):
        swapped(d).wait_recv()
    for d in range(1, groups):
        swap(d).wait_send()
    for s in range(1, n):
        for copy in line(s):
            copy.wait_send()


def reduce_rows(n, groups, part, tile):
    own_rows, blocks = part.shape[2:]
    dma = pltpu.SemaphoreType.DMA
    shape = (groups, own_rows, blocks)
    return pl.pallas_call(
        functools.partial(reduce_kernel, n, groups),
        name="reduce_rows",
        out_shape=(jax.ShapeDtypeStruct(shape, part.dtype), jax.ShapeDtypeStruct(tile.shape, tile.dtype)),
        in_specs=[VMEM] * 2,
        out_specs=(VMEM,) * 2,
        scratch_shapes=[
            pltpu.VMEM((n - 1,) + shape, part.dtype), pltpu.VMEM((n - 1,) + tile.shape, tile.dtype),
            pltpu.VMEM(shape, part.dtype),
            dma((n - 1,)), dma((n - 1,)), dma((n - 1,)), dma((n - 1,)), dma((groups - 1,)), dma((groups - 1,)),
        ],
        compiler_params=pltpu.CompilerParams(collective_id=2, has_side_effects=True),
    )(part, tile)


def body(tokens, targets, live_mask, up_weight, down_weight, probe_rows, probe_cols, moment):
    tok_count, features = tokens.shape
    own_rows, ff_held = up_weight.shape
    n, groups, cores = lax.axis_size("hi"), lax.axis_size("lo"), lax.axis_size("tensor")
    cols = ff_held // groups
    share = tok_count // cores
    col_keys = lax.dynamic_slice_in_dim(probe_cols, lax.axis_index("lo") * cols, cols)
    signs = probe_signs(probe_rows, col_keys)
    first = lax.axis_index("tensor") * share
    live_own = lax.dynamic_slice_in_dim(live_mask, first, share).astype(jnp.float32)[:, None]
    targets_own = lax.dynamic_slice_in_dim(targets, first, share)
    all_tokens, up_full, down_full = gather(n, groups, tokens, up_weight, down_weight)
    all_tokens = all_tokens.reshape(-1, features)
    up_full = up_full.reshape(features, cols)
    down_full = down_full.reshape(features, cols)
    preact = jnp.dot(all_tokens, up_full, preferred_element_type=jnp.float32)
    tangent = jnp.dot(all_tokens, signs, preferred_element_type=jnp.float32)
    gelu_value, gelu_slope, gelu_curve = gelu_parts(preact)
    hidden = gelu_value.astype(jnp.bfloat16)
    hidden_dir = (gelu_slope * tangent).astype(jnp.bfloat16)
    dims = (((1,), (1,)), ((), ()))
    out_part = lax.dot_general(hidden, down_full, dims, preferred_element_type=jnp.float32).astype(jnp.bfloat16)
    dir_part = lax.dot_general(hidden_dir, down_full, dims, preferred_element_type=jnp.float32)
    split = (groups, cores, share, features)
    residual, tiles = exchange(groups, cores, out_part.reshape(split), dir_part.reshape(split), targets_own, live_own)
    residual = residual.reshape(2, -1, features)
    tile = jnp.sum(tiles, axis=(0, 1))
    grads = jnp.einsum("ntd,df->ntf", residual, down_full, preferred_element_type=jnp.float32)
    chain_grad = (grads[1] * gelu_slope + grads[0] * gelu_curve * tangent).astype(jnp.bfloat16)
    product = jnp.einsum("tr,tf->rf", all_tokens, chain_grad, preferred_element_type=jnp.float32)
    blocks = cols // BLOCK
    member = (
        lax.broadcasted_iota(jnp.int32, (cols, blocks), 0) // BLOCK
        == lax.broadcasted_iota(jnp.int32, (cols, blocks), 1)
    ).astype(jnp.float32)
    summed = jnp.dot(signs.astype(jnp.float32) * product, member, precision=lax.Precision.HIGH)
    rows, sums = reduce_rows(n, groups, summed.reshape(n, groups, own_rows, blocks), tile)
    loss_sum, total_count = sums[0, 0], sums[1, 0]
    summed = rows.transpose(1, 0, 2).reshape(own_rows, groups * blocks)
    hess_diag = summed * (1.0 / BLOCK) / total_count
    second_moment = beta_two * moment + (1.0 - beta_two) * hess_diag * hess_diag
    mean_loss = loss_sum / (2.0 * total_count)
    return (hess_diag, second_moment, mean_loss)


def solution(mesh):
    dp = mesh.shape["dp"]
    lo = math.gcd(dp, 4)
    split = Mesh(mesh.devices.reshape(dp // lo, lo, mesh.shape["tensor"]), ("hi", "lo", "tensor"))
    rows = ("hi", "lo")
    placed = (
        P(rows, None),
        P(rows, None),
        P(rows),
        P(rows, "tensor"),
        P(rows, "tensor"),
        P(),
        P("tensor"),
        P(rows, "tensor"),
    )
    return jax.shard_map(
        body,
        mesh=split,
        in_specs=placed,
        out_specs=(P(rows, "tensor"), P(rows, "tensor"), P()),
        check_vma=False,
    )
```

time: 397 us -> 257 us (0.65)
  Pallas kernels: 0 us -> 208 us
  waiting for transfers between devices: 196 us -> 0 us
  blocking collectives: 125 us -> 0 us
  between operations: 16.5 us -> 3.13 us
  matrix products: 25.3 us -> 36.2 us
  local copies, waits for them, and re-layouts: 14.8 us -> 5.18 us
  starting transfers between devices: 8.39 us -> 0 us
  other arithmetic: 9.84 us -> 2.25 us
    pallas_call x0 -> x3, Pallas kernels: none -> 208 us  [the longest x1 118 us: gather(): pl.pallas_call(functools.partial(gather_kernel, n, groups), name='gather'...]
    all_gather x4 -> x0, waiting for transfers between devices: 113 us -> none  [the longest x2 72.7 us: spread(): full = lax.all_gather(pieces, TKX, axis=1 if FFX == 'hi' else 0)]
    all_to_all x3 -> x0, blocking collectives: 85.4 us -> none  [the longest x2 73 us: spread(): lax.all_to_all(weight.reshape(own_rows, groups, cols), FFX, split_axis=1,...]
    all_to_all x2 -> x0, waiting for transfers between devices: 81.9 us -> none  [the longest x1 81.9 us: body(): part = lax.all_to_all(part, (FFX, 'tensor'), split_axis=1, concat_axis=0)]
    psum x1 -> x0, blocking collectives: 39.8 us -> none  [body(): lax.psum(jnp.stack([jnp.sum(weighted * diff), jnp.sum(live_own)]), everyone)]
    all_to_all x2 -> x0, starting transfers between devices: 8.05 us -> none  [the longest x1 4.73 us: body(): part = lax.all_to_all(part, (FFX, 'tensor'), split_axis=1, concat_axis=0)]
    another operation x7 -> x0, local copies, waits for them, and re-layouts: 5.07 us -> none  [the longest x4 2.19 us: spread(): lax.all_to_all(weight.reshape(own_rows, groups, cols), FFX, split_axis=1,...]
    another operation x4 -> x0, other arithmetic: 4.84 us -> none  [the longest x1 2.56 us: body(): stacked = jnp.stack([hidden, hidden_dir])]
  transfers between devices with their start and end apart: 6 -> 0, of which waited for: 4 -> 0; matrix products, arithmetic and copies ran while one was open for 4% -> 0% of each run, Pallas kernels for 0% -> 0%
where the time goes in v2:
time: 257 us; the launch traced here: 255 us
  Pallas kernels  208 us (81%)
  matrix products  36.2 us (14%)
  local copies, waits for them, and re-layouts  5.18 us (2%)
  between operations  3.13 us (1%)
    pallas_call x1, Pallas kernels, gather(): pl.pallas_call(functools.partial(gather_kernel, n, groups), name='gather'...  118 us
    pallas_call x1, Pallas kernels, exchange(): pl.pallas_call(functools.partial(residual_kernel, groups, cores), name='r...  64.6 us
    pallas_call x1, Pallas kernels, reduce_rows(): pl.pallas_call(functools.partial(reduce_kernel, n, groups), name='reduce_...  25.8 us
    dot_general x1, matrix products, body(): tangent = jnp.dot(all_tokens, signs, preferred_element_type=jnp.float32)  7.58 us
    dot_general x1, matrix products, body(): jnp.einsum('ntd,df->ntf', residual, down_full, preferred_element_type=jnp...  7.1 us
    dot_general x1, matrix products, body(): preact = jnp.dot(all_tokens, up_full, preferred_element_type=jnp.float32)  5.88 us
    dot_general x1, matrix products, body(): jnp.dot(signs.astype(jnp.float32) * product, member, precision=lax.Precis...  5.32 us

profile of v2, /device:TPU:0, one launch (start us, length us, event | category | flops | bytes accessed | tf_op | source)
XLA Modules:
  0.0 254.9 jit_solution(12749854931420264759)
XLA Ops:
  0.6 0.0 copy-start
  0.6 117.8 %gather.1 = (bf16[4,128,1792]{2,1,0:T(8,128)(2,1)}, bf16[4,4,112,896]{3,2,1,0:T(8,128)(2,1)}, bf16[4,4,112,896]{3,2,1,0:T(8,128)(2,1)}) custom-call(bf16[128,1792]{1,0:T(8,128)(2,1)} %tok_ref.1, bf16[112,3584]{1,0:T(8,128)(2,1)} %up_ref.1, bf16[112,3584]{1,0:T(8,128)(2,1)} %down_ref.1), custom_call_target="tpu_custom_call" | custom-call | tf_op jit(solution)/shard_map/gather/pallas_call | solution.py:161
  118.5 0.0 copy-start.3
  118.5 5.9 %fusion.69 = f32[512,896]{1,0:T(8,128)} fusion(bf16[512,1792]{1,0:T(8,128)(2,1)} %bitcast.50, bf16[1792,896]{1,0:T(8,128)(2,1)} %bitcast.49), kind=kOutput, calls=%fused_computation.91 | convolution fusion | flops 1644167168 | bytes 6881280 | tf_op jit(solution)/shard_map/dot_general | solution.py:388
  124.4 0.8 dynamic_slice.9
  125.2 0.0 copy-done.3
  125.2 7.6 %multiply_convert_fusion = (bf16[512,896]{1,0:T(8,128)(2,1)S(1)}, f32[512,896]{1,0:T(8,128)}) fusion(f32[512,896]{1,0:T(8,128)} %fusion.69, bf16[512,1792]{1,0:T(8,128)(2,1)S(1)} %bitcast.51, s32[896]{0:T(1024)S(1)} %dynamic_slice.9, s32[1792]{0:T(1024)S(1)} %broadcast_multiply_fusion), kind=kOutput, calls=%fused_computation.30 | convolution fusion | flops 1680179200 | bytes 6433280 | tf_op jit(solution)/shard_map/dot_general | solution.py:389
  132.8 3.6 %convolution_convert_fusion = bf16[512,1792]{1,0:T(8,128)(2,1)} fusion(bf16[1792,896]{1,0:T(8,128)(2,1)S(1)} %bitcast.47, f32[512,896]{1,0:T(8,128)S(1)} %copy-done.7), kind=kOutput, calls=%fused_computation.13 | convolution fusion | flops 1649213440 | bytes 6881280 | tf_op jit(solution)/shard_map/dot_general | solution.py:394
  136.4 3.9 %fusion.70.dir_ref = f32[4,2,64,1792]{3,2,1,0:T(8,128)} fusion(bf16[4,2,64,896]{3,2,1,0:T(8,128)(2,1)S(1)} %bitcast.53, bf16[1792,896,1,1]{1,0,3,2:T(8,128)(2,1)S(1)} %bitcast.48), kind=kOutput, calls=%fused_computation.92 | convolution fusion | flops 1644167168 | bytes 7798784 | tf_op jit(solution)/shard_map/dot_general | solution.py:395
  140.3 0.7 constant_dynamic-slice_fusion.targets_ref
  141.0 0.1 convert_bitcast_fusion
  141.1 0.7 copy.13.live_ref
  141.8 64.6 %residual.1 = (bf16[2,4,2,64,1792]{4,3,2,1,0:T(8,128)(2,1)}, f32[4,2,8,128]{3,2,1,0:T(8,128)}) custom-call(bf16[4,2,64,1792]{3,2,1,0:T(8,128)(2,1)} %bitcast.42, f32[4,2,64,1792]{3,2,1,0:T(8,128)} %fusion.70.dir_ref, bf16[64,1792]{1,0:T(8,128)(2,1)} %constant_dynamic-slice_fusion.targets_ref, f32[64,1]{1,0:T(8,128)} %copy.13.live_ref), custom_call_target="tpu_custom_call" | custom-call | tf_op jit(solution)/shard_map/residual/pallas_call | solution.py:282
  206.4 7.1 %fusion.71 = f32[2,512,896]{2,1,0:T(8,128)S(1)} fusion(bf16[2,512,1792]{2,1,0:T(8,128)(2,1)} %bitcast.45, bf16[1792,896,1]{1,0,2:T(8,128)(2,1)} %bitcast.46), kind=kOutput, calls=%fused_computation.93 | convolution fusion | flops 3288334336 | bytes 10551296 | tf_op jit(solution)/shard_map/ntd,df->ntf/dot_general | solution.py:400
  213.6 2.8 %fusion.25 = f32[1792,896]{1,0:T(8,128)S(1)} fusion(bf16[512,1792]{1,0:T(8,128)(2,1)S(1)} %bitcast.52, f32[512,896]{1,0:T(8,128)S(1)} %copy-done.9, f32[2,512,896]{2,1,0:T(8,128)S(1)} %fusion.71, f32[512,896]{1,0:T(8,128)S(1)} %copy-done.8), kind=kOutput, calls=%fused_computation.38 | convolution fusion | flops 1657929728 | bytes 15597568 | tf_op jit(solution)/shard_map/tr,tf->rf/dot_general | solution.py:402
  216.4 5.3 %fusion.6 = f32[1792,64]{1,0:T(8,128)} fusion(f32[1792,896]{1,0:T(8,128)S(1)} %fusion.25, s32[896]{0:T(1024)S(1)} %dynamic_slice.9, s32[1792]{0:T(1024)S(1)} %broadcast_multiply_fusion, s32[896]{0:T(1024)S(1)} %get-tuple-element.24, s32[896]{0:T(1024)S(1)} %get-tuple-element.25, pred[896]{0:T(1024)(128)(4,1)S(1)} %fusion.33), kind=kOutput, calls=%fused_computation.8 | convolution fusion | flops 647184384 | bytes 6900096 | tf_op jit(solution)/shard_map/dot_general | solution.py:408
  221.7 0.6 reduce_sum.9.tile_ref
  222.3 25.8 %reduce_rows.1 = (f32[4,112,64]{2,1,0:T(8,128)}, f32[8,128]{1,0:T(8,128)}) custom-call(f32[4,4,112,64]{3,2,1,0:T(8,128)} %bitcast.44, f32[8,128]{1,0:T(8,128)} %reduce_sum.9.tile_ref), custom_call_target="tpu_custom_call" | custom-call | tf_op jit(solution)/shard_map/reduce_rows/pallas_call | solution.py:358
  248.1 1.3 fusion.68
  249.3 1.5 divide_bitcast_fusion
  250.9 0.1 copy.15
  251.0 0.8 copy.17
  251.7 0.1 copy.16
  251.9 0.7 copy.18
  (21 shorter events, 0.1 us)
Async XLA Ops:
  0.6 139.7 %copy-start = (bf16[128,1792]{1,0:T(8,128)(2,1)S(1)}, bf16[128,1792]{1,0:T(8,128)(2,1)}, u32[]{:S(2)}) copy-start(bf16[128,1792]{1,0:T(8,128)(2,1)} %param.9) | copy-start | bytes 1376260
  118.5 6.7 %copy-start.3 = (s32[1792]{0:T(1024)S(1)}, s32[1792]{0:T(1024)}, u32[]{:S(2)}) copy-start(s32[1792]{0:T(1024)} %param.13) | copy-start | bytes 21508
  118.5 6.7 %copy-start.5 = (bf16[4,128,1792]{2,1,0:T(8,128)(2,1)S(1)}, bf16[4,128,1792]{2,1,0:T(8,128)(2,1)}, u32[]{:S(2)}) copy-start(bf16[4,128,1792]{2,1,0:T(8,128)(2,1)} %get-tuple-element.10) | copy-start | bytes 5505028
  125.2 7.6 %copy-start.4 = (bf16[4,4,112,896]{3,2,1,0:T(8,128)(2,1)S(1)}, bf16[4,4,112,896]{3,2,1,0:T(8,128)(2,1)}, u32[]{:S(2)}) copy-start(bf16[4,4,112,896]{3,2,1,0:T(8,128)(2,1)} %get-tuple-element.12) | copy-start | bytes 9633796
  125.2 7.6 %copy-start.7 = (f32[512,896]{1,0:T(8,128)S(1)}, f32[512,896]{1,0:T(8,128)}, u32[]{:S(2)}) copy-start(f32[512,896]{1,0:T(8,128)} %fusion.69) | copy-start | bytes 5505028
  136.4 4.6 %copy-start.6 = (s32[128]{0:T(128)S(1)}, s32[128]{0:T(128)}, u32[]{:S(2)}) copy-start(s32[128]{0:T(128)} %param.10) | copy-start | bytes 1540
  206.4 7.1 %copy-start.8 = (f32[512,896]{1,0:T(8,128)S(1)}, f32[512,896]{1,0:T(8,128)}, u32[]{:S(2)}) copy-start(f32[512,896]{1,0:T(8,128)} %fusion.69) | copy-start | bytes 5505028
  206.4 7.1 %copy-start.9 = (f32[512,896]{1,0:T(8,128)S(1)}, f32[512,896]{1,0:T(8,128)}, u32[]{:S(2)}) copy-start(f32[512,896]{1,0:T(8,128)} %get-tuple-element.23) | copy-start | bytes 5505028
  216.4 5.3 %copy-start.2 = (f32[4,2,8,128]{3,2,1,0:T(8,128)S(1)}, f32[4,2,8,128]{3,2,1,0:T(8,128)}, u32[]{:S(2)}) copy-start(f32[4,2,8,128]{3,2,1,0:T(8,128)} %get-tuple-element.14) | copy-start | bytes 98308
  221.7 30.0 %copy-start.1 = (f32[112,256]{1,0:T(8,128)S(1)}, f32[112,256]{1,0:T(8,128)}, u32[]{:S(2)}) copy-start(f32[112,256]{1,0:T(8,128)} %param.15) | copy-start | bytes 344068

commit v3 on v2

v3 whole, which is shorter than its diff:
```python
import functools
import jax
import jax.numpy as jnp
from jax import lax
from jax.experimental import pallas as pl
from jax.experimental.pallas import tpu as pltpu
from jax.sharding import Mesh, PartitionSpec as P

BLOCK = 14

gelu_coef = 0.7978845608028654
cubic_coef = 0.044715
beta_two = 0.999


def probe_signs(row_keys, col_keys):
    hashed = jnp.bitwise_xor(row_keys[:, None] * 747796405, col_keys[None, :])
    hashed = jnp.bitwise_xor(hashed, jnp.right_shift(hashed, 15) & 131071)
    hashed = hashed * 695872825
    hashed = jnp.bitwise_xor(hashed, jnp.right_shift(hashed, 13) & 524287)
    hashed = hashed * 739982445
    hashed = jnp.bitwise_xor(hashed, jnp.right_shift(hashed, 16) & 65535)
    parity = jnp.right_shift(hashed, 11) & 1
    return (2 * parity - 1).astype(jnp.bfloat16)


def gelu_parts(preact):
    tanh_arg = gelu_coef * (preact + cubic_coef * preact * preact * preact)
    tanh_val = jnp.tanh(tanh_arg)
    sech_sq = 1.0 - tanh_val * tanh_val
    arg_slope = gelu_coef * (1.0 + 3.0 * cubic_coef * preact * preact)
    arg_curve = gelu_coef * 6.0 * cubic_coef * preact
    gelu_value = 0.5 * preact * (1.0 + tanh_val)
    gelu_slope = 0.5 * (1.0 + tanh_val) + 0.5 * preact * sech_sq * arg_slope
    gelu_curve = sech_sq * (
        arg_slope - preact * tanh_val * arg_slope * arg_slope + 0.5 * preact * arg_curve
    )
    return (gelu_value, gelu_slope, gelu_curve)


AXES = ("a", "b", "e", "f", "tensor")
MESH = pl.DeviceIdType.MESH
ANY = pl.BlockSpec(memory_space=pl.ANY)
VMEM = pl.BlockSpec(memory_space=pltpu.VMEM)


def remote(src, dst, send_sem, recv_sem, device):
    return pltpu.make_async_remote_copy(
        src_ref=src, dst_ref=dst, send_sem=send_sem, recv_sem=recv_sem, device_id=device, device_id_type=MESH
    )


def offsets(*sizes):
    found = [()]
    for size in sizes:
        found = [head + (step,) for head in found for step in range(size)]
    return found


def moved(at, step, size, way):
    return lax.rem(at + step if way > 0 else at + size - step, size)


def gather_kernel(
    sizes, tok_ref, up_ref, down_ref, tok_all, up_all, down_all,
    own_sem, tok_send, tok_recv, swap_send, swap_recv, far_send, far_recv, near_send, near_recv,
):
    na, nb, ne, nf = sizes
    a, b, e, f, c = (lax.axis_index(name) for name in AXES)
    cols = up_all.shape[5]
    plane = offsets(nb, nf)
    barrier = pltpu.get_barrier_semaphore()

    def peer(d, way):
        return (a, moved(b, plane[d][0], nb, way), e, moved(f, plane[d][1], nf, way), c)

    def far(s, way):
        return (moved(a, s, na, way), b, e, f, c)

    def near(t, way):
        return (a, b, moved(e, t, ne, way), f, c)

    friends = [peer(d, 1) for d in range(1, len(plane))]
    friends += [far(s, 1) for s in range(1, na)] + [near(t, 1) for t in range(1, ne)]
    for place in friends:
        pl.semaphore_signal(barrier, inc=1, device_id=place, device_id_type=MESH)
    pl.semaphore_wait(barrier, len(friends))

    held = ((up_ref, up_all), (down_ref, down_all))

    def cut(w, place):
        return held[w][0].at[:, pl.ds(pl.multiple_of((place[1] * nf + place[3]) * cols, cols), cols)]

    def swap(w, d):
        to = peer(d, 1)
        sems = swap_send.at[w, d - 1], swap_recv.at[w, d - 1]
        return remote(cut(w, to), held[w][1].at[a, b, e, f], *sems, to)

    def swapped(w, d):
        came = peer(d, -1)
        sems = swap_send.at[w, d - 1], swap_recv.at[w, d - 1]
        return remote(cut(w, came), held[w][1].at[a, came[1], e, came[3]], *sems, came)

    def token(d, way):
        place = peer(d, way)
        slot = tok_all.at[b, f] if way > 0 else tok_all.at[place[1], place[3]]
        return remote(tok_ref, slot, tok_send.at[d - 1], tok_recv.at[d - 1], place)

    def chunk(w, d, at_a, at_e):
        came = peer(d, -1)
        return held[w][1].at[at_a, came[1], at_e, came[3]]

    def far_hop(w, d, s, way):
        slot = chunk(w, d, a if way > 0 else moved(a, s, na, -1), e)
        return remote(slot, slot, far_send.at[w, d, s - 1], far_recv.at[w, d, s - 1], far(s, way))

    def near_hop(w, d, s, t, way):
        slot = chunk(w, d, moved(a, s, na, -1), e if way > 0 else moved(e, t, ne, -1))
        return remote(slot, slot, near_send.at[w, d, s, t - 1], near_recv.at[w, d, s, t - 1], near(t, way))

    owns = [pltpu.make_async_copy(cut(w, (a, b, e, f)), held[w][1].at[a, b, e, f], own_sem.at[w]) for w in range(2)]
    owns.append(pltpu.make_async_copy(tok_ref, tok_all.at[b, f], own_sem.at[2]))
    for copy in owns:
        copy.start()
    for d in range(1, len(plane)):
        swap(0, d).start()
    for d in range(1, len(plane)):
        swap(1, d).start()
    for d in range(1, len(plane)):
        token(d, 1).start()
    for w in range(2):
        for d in range(len(plane)):
            if d == 0:
                owns[w].wait()
            else:
                swapped(w, d).wait_recv()

            @pl.loop(1, na)
            def _(s):
                far_hop(w, d, s, 1).start()

            for t in range(1, ne):
                near_hop(w, d, 0, t, 1).start()
    for w in range(2):
        for d in range(len(plane)):
            @pl.loop(1, na)
            def _(s):
                far_hop(w, d, s, -1).wait_recv()
                for t in range(1, ne):
                    near_hop(w, d, s, t, 1).start()

    owns[2].wait()
    for d in range(1, len(plane)):
        token(d, -1).wait_recv()
        token(d, 1).wait_send()
    for w in range(2):
        for d in range(1, len(plane)):
            swap(w, d).wait_send()
        for d in range(len(plane)):
            @pl.loop(0, na)
            def _(s):
                for t in range(1, ne):
                    near_hop(w, d, s, t, -1).wait_recv()
                    near_hop(w, d, s, t, 1).wait_send()

            @pl.loop(1, na)
            def _(s):
                far_hop(w, d, s, 1).wait_send()


def gather(sizes, tokens, up_weight, down_weight):
    na, nb, ne, nf = sizes
    tok_count, features = tokens.shape
    own_rows, ff_held = up_weight.shape
    groups = nb * nf
    full = jax.ShapeDtypeStruct(sizes + (own_rows, ff_held // groups), up_weight.dtype)
    dma = pltpu.SemaphoreType.DMA
    return pl.pallas_call(
        functools.partial(gather_kernel, sizes),
        name="gather",
        out_shape=(jax.ShapeDtypeStruct((nb, nf, tok_count, features), tokens.dtype), full, full),
        in_specs=[ANY] * 3,
        out_specs=(ANY,) * 3,
        scratch_shapes=[
            dma((3,)), dma((groups - 1,)), dma((groups - 1,)), dma((2, groups - 1)), dma((2, groups - 1)),
            dma((2, groups, na - 1)), dma((2, groups, na - 1)),
            dma((2, groups, na, ne - 1)), dma((2, groups, na, ne - 1)),
        ],
        compiler_params=pltpu.CompilerParams(collective_id=0, has_side_effects=True),
    )(tokens, up_weight, down_weight)


def residual_kernel(
    sizes, cores, out_ref, dir_ref, targets_ref, live_ref, res_all, tile_all,
    half_out, half_dir, send_out, send_dir, got_out, got_dir,
    half_send, half_recv, part_send, part_recv, res_send, res_recv, pass_send, pass_recv, tile_send, tile_recv,
):
    na, nb, ne, nf = sizes
    a, b, e, f, c = (lax.axis_index(name) for name in AXES)
    plane = offsets(nb, nf)
    groups = len(plane)
    twin = 1 - c
    g = b * nf + f
    twin_at = (a, b, e, f, twin)
    barrier = pltpu.get_barrier_semaphore()
    others = [(d, k) for d in range(groups) for k in range(cores) if (d, k) != (0, 0)]

    def at(d, k, way=1):
        return (a, moved(b, plane[d][0], nb, way), e, moved(f, plane[d][1], nf, way), moved(c, k, cores, way))

    def back(d, k):
        return at(d, k, -1)

    def spot(d, way):
        place = at(d, 0, way)
        return place[1] * nf + place[3]

    for d, k in others:
        pl.semaphore_signal(barrier, inc=1, device_id=at(d, k), device_id_type=MESH)
    pl.semaphore_wait(barrier, len(others))

    def halves(d):
        to = spot(d, 1)
        return (
            remote(out_ref.at[to, twin], half_out.at[d], half_send.at[0, d], half_recv.at[0, d], twin_at),
            remote(dir_ref.at[to, twin], half_dir.at[d], half_send.at[1, d], half_recv.at[1, d], twin_at),
        )

    def parts(d):
        return (
            remote(send_out.at[d], got_out.at[d - 1], part_send.at[0, d - 1], part_recv.at[0, d - 1], at(d, 0)),
            remote(send_dir.at[d], got_dir.at[d - 1], part_send.at[1, d - 1], part_recv.at[1, d - 1], at(d, 0)),
        )

    order = list(range(1, groups)) + [0]
    for d in order:
        for copy in halves(d):
            copy.start()
    for d in order:
        to = spot(d, 1)
        for copy in halves(d):
            copy.wait_recv()
        total = out_ref[to, c].astype(jnp.float32) + half_out[d].astype(jnp.float32)
        send_out[d] = total.astype(jnp.bfloat16)
        send_dir[d] = dir_ref[to, c] + half_dir[d]
        if d:
            for copy in parts(d):
                copy.start()
    outputs = total
    out_dir = send_dir[0]
    for d in range(1, groups):
        for copy in parts(d):
            copy.wait_recv()
        outputs += got_out[d - 1].astype(jnp.float32)
        out_dir += got_dir[d - 1]
    live = live_ref[...]
    diff = outputs - targets_ref[...].astype(jnp.float32)
    weighted = live * diff
    res_all[0, g, c] = weighted.astype(jnp.bfloat16)
    res_all[1, g, c] = (live * out_dir).astype(jnp.bfloat16)
    loss = jnp.sum(weighted * diff, keepdims=True)
    count = jnp.sum(live, keepdims=True)
    tile_all[g, c] = jnp.where(lax.broadcasted_iota(jnp.int32, tile_all.shape[2:], 0) == 0, loss, count)

    def sent(d):
        slot = res_all.at[:, g, c]
        return remote(slot, slot, res_send.at[d], res_recv.at[d], at(d, 0) if d else twin_at)

    def received(d):
        slot = res_all.at[:, spot(d, -1), c] if d else res_all.at[:, g, twin]
        return remote(slot, slot, res_send.at[d], res_recv.at[d], back(d, 0) if d else twin_at)

    def passed(d, core):
        slot = res_all.at[:, spot(d, -1), core]
        return remote(slot, slot, pass_send.at[d - 1], pass_recv.at[d - 1], twin_at)

    def tile(i, source, place):
        slot = tile_all.at[source[1] * nf + source[3], source[4]]
        return remote(slot, slot, tile_send.at[i], tile_recv.at[i], place)

    for d in order:
        sent(d).start()
    for i, (d, k) in enumerate(others):
        tile(i, (a, b, e, f, c), at(d, k)).start()
    for d in range(1, groups):
        received(d).wait_recv()
        passed(d, c).start()
    received(0).wait_recv()
    for i, (d, k) in enumerate(others):
        tile(i, back(d, k), back(d, k)).wait_recv()
    for d in range(1, groups):
        passed(d, twin).wait_recv()
    for d in range(groups):
        for copy in halves(d):
            copy.wait_send()
        sent(d).wait_send()
        if d:
            for copy in parts(d):
                copy.wait_send()
            passed(d, c).wait_send()
    for i, (d, k) in enumerate(others):
        tile(i, (a, b, e, f, c), at(d, k)).wait_send()


def exchange(sizes, cores, out_part, dir_part, targets, live):
    groups = sizes[1] * sizes[3]
    share, features = targets.shape
    dma = pltpu.SemaphoreType.DMA
    bf, f32 = jnp.bfloat16, jnp.float32
    return pl.pallas_call(
        functools.partial(residual_kernel, sizes, cores),
        name="residual",
        out_shape=(
            jax.ShapeDtypeStruct((2, groups, cores, share, features), bf),
            jax.ShapeDtypeStruct((groups, cores, 8, 128), f32),
        ),
        in_specs=[VMEM] * 4,
        out_specs=(VMEM,) * 2,
        scratch_shapes=[
            pltpu.VMEM((groups, share, features), bf), pltpu.VMEM((groups, share, features), f32),
            pltpu.VMEM((groups, share, features), bf), pltpu.VMEM((groups, share, features), f32),
            pltpu.VMEM((groups - 1, share, features), bf), pltpu.VMEM((groups - 1, share, features), f32),
            dma((2, groups)), dma((2, groups)), dma((2, groups - 1)), dma((2, groups - 1)),
            dma((groups,)), dma((groups,)), dma((groups - 1,)), dma((groups - 1,)),
            dma((groups * cores - 1,)), dma((groups * cores - 1,)),
        ],
        compiler_params=pltpu.CompilerParams(collective_id=1, has_side_effects=True),
    )(out_part, dir_part, targets, live)


def reduce_kernel(
    sizes, part_ref, tile_ref, out_ref, sums_ref, got, got_tile, total,
    line_send, line_recv, tile_send, tile_recv, swap_send, swap_recv,
):
    na, nb, ne, nf = sizes
    a, b, e, f, c = (lax.axis_index(name) for name in AXES)
    plane, fans = offsets(nb, nf), offsets(na, ne)
    barrier = pltpu.get_barrier_semaphore()

    def peer(d, way):
        return (a, moved(b, plane[d][0], nb, way), e, moved(f, plane[d][1], nf, way), c)

    def fan(s):
        return (moved(a, fans[s][0], na, 1), b, moved(e, fans[s][1], ne, 1), f, c)

    friends = [peer(d, 1) for d in range(1, len(plane))] + [fan(s) for s in range(1, len(fans))]
    for place in friends:
        pl.semaphore_signal(barrier, inc=1, device_id=place, device_id_type=MESH)
    pl.semaphore_wait(barrier, len(friends))

    def line(s):
        to = fan(s)
        return (
            remote(part_ref.at[to[0], :, to[2]], got.at[s - 1], line_send.at[s - 1], line_recv.at[s - 1], to),
            remote(tile_ref, got_tile.at[s - 1], tile_send.at[s - 1], tile_recv.at[s - 1], to),
        )

    def swap(d, way):
        place = peer(d, way)
        slot = out_ref.at[b, f] if way > 0 else out_ref.at[place[1], place[3]]
        return remote(total.at[place[1], place[3]], slot, swap_send.at[d - 1], swap_recv.at[d - 1], place)

    for s in range(1, len(fans)):
        for copy in line(s):
            copy.start()
    acc = part_ref[a, :, e]
    sums = tile_ref[...]
    for s in range(1, len(fans)):
        for copy in line(s):
            copy.wait_recv()
        acc += got[s - 1]
        sums += got_tile[s - 1]
    total[...] = acc
    sums_ref[...] = sums
    for d in range(1, len(plane)):
        swap(d, 1).start()
    out_ref[b, f] = total[b, f]
    for d in range(1, len(plane)):
        swap(d, -1).wait_recv()
    for d in range(1, len(plane)):
        swap(d, 1).wait_send()
    for s in range(1, len(fans)):
        for copy in line(s):
            copy.wait_send()


def reduce_rows(sizes, part, tile):
    na, nb, ne, nf = sizes
    dma = pltpu.SemaphoreType.DMA
    shape = (nb, nf) + part.shape[4:]
    peers, groups = na * ne - 1, nb * nf
    return pl.pallas_call(
        functools.partial(reduce_kernel, sizes),
        name="reduce_rows",
        out_shape=(jax.ShapeDtypeStruct(shape, part.dtype), jax.ShapeDtypeStruct(tile.shape, tile.dtype)),
        in_specs=[VMEM] * 2,
        out_specs=(VMEM,) * 2,
        scratch_shapes=[
            pltpu.VMEM((peers,) + shape, part.dtype), pltpu.VMEM((peers,) + tile.shape, tile.dtype),
            pltpu.VMEM(shape, part.dtype),
            dma((peers,)), dma((peers,)), dma((peers,)), dma((peers,)), dma((groups - 1,)), dma((groups - 1,)),
        ],
        compiler_params=pltpu.CompilerParams(collective_id=2, has_side_effects=True),
    )(part, tile)


def body(tokens, targets, live_mask, up_weight, down_weight, probe_rows, probe_cols, moment):
    tok_count, features = tokens.shape
    own_rows, ff_held = up_weight.shape
    *sizes, cores = (lax.axis_size(name) for name in AXES)
    sizes = tuple(sizes)
    groups = sizes[1] * sizes[3]
    cols = ff_held // groups
    share = tok_count // cores
    col_keys = lax.dynamic_slice_in_dim(probe_cols, lax.axis_index(("b", "f")) * cols, cols)
    signs = probe_signs(probe_rows, col_keys)
    first = lax.axis_index("tensor") * share
    live_own = lax.dynamic_slice_in_dim(live_mask, first, share).astype(jnp.float32)[:, None]
    targets_own = lax.dynamic_slice_in_dim(targets, first, share)
    all_tokens, up_full, down_full = gather(sizes, tokens, up_weight, down_weight)
    all_tokens = all_tokens.reshape(-1, features)
    up_full = up_full.reshape(features, cols)
    down_full = down_full.reshape(features, cols)
    preact = jnp.dot(all_tokens, up_full, preferred_element_type=jnp.float32)
    tangent = jnp.dot(all_tokens, signs, preferred_element_type=jnp.float32)
    gelu_value, gelu_slope, gelu_curve = gelu_parts(preact)
    hidden = gelu_value.astype(jnp.bfloat16)
    hidden_dir = (gelu_slope * tangent).astype(jnp.bfloat16)
    dims = (((1,), (1,)), ((), ()))
    out_part = lax.dot_general(hidden, down_full, dims, preferred_element_type=jnp.float32).astype(jnp.bfloat16)
    dir_part = lax.dot_general(hidden_dir, down_full, dims, preferred_element_type=jnp.float32)
    split = (groups, cores, share, features)
    residual, tiles = exchange(sizes, cores, out_part.reshape(split), dir_part.reshape(split), targets_own, live_own)
    residual = residual.reshape(2, -1, features)
    tile = jnp.sum(tiles, axis=(0, 1))
    grads = jnp.einsum("ntd,df->ntf", residual, down_full, preferred_element_type=jnp.float32)
    chain_grad = (grads[1] * gelu_slope + grads[0] * gelu_curve * tangent).astype(jnp.bfloat16)
    product = jnp.einsum("tr,tf->rf", all_tokens, chain_grad, preferred_element_type=jnp.float32)
    blocks = cols // BLOCK
    row_halves = 2 if own_rows % 2 == 0 else 1
    column = lax.broadcasted_iota(jnp.int32, (cols, row_halves * blocks), 1)
    owner = lax.broadcasted_iota(jnp.int32, (cols, row_halves * blocks), 0) // BLOCK
    signed = (signs.astype(jnp.float32) * product).reshape(-1, row_halves, own_rows // row_halves, cols)
    summed = 0.0
    for half in range(row_halves):
        member = (owner + half * blocks == column).astype(jnp.float32)
        summed += jnp.einsum("hrf,fk->hrk", signed[:, half], member, precision=lax.Precision.HIGH)
    rows, sums = reduce_rows(sizes, summed.reshape(sizes + summed.shape[1:]), tile)
    loss_sum, total_count = sums[0, 0], sums[1, 0]
    summed = rows.reshape(groups, own_rows // row_halves, row_halves, blocks)
    summed = summed.transpose(2, 1, 0, 3).reshape(own_rows, groups * blocks)
    hess_diag = summed * (1.0 / BLOCK) / total_count
    second_moment = beta_two * moment + (1.0 - beta_two) * hess_diag * hess_diag
    mean_loss = loss_sum / (2.0 * total_count)
    return (hess_diag, second_moment, mean_loss)


def solution(mesh):
    dp = mesh.shape["dp"]
    cuts = (dp // 8, 2, 2, 2)
    split = Mesh(mesh.devices.reshape(cuts + (mesh.shape["tensor"],)), AXES)
    rows = AXES[:4]
    placed = (
        P(rows, None),
        P(rows, None),
        P(rows),
        P(rows, "tensor"),
        P(rows, "tensor"),
        P(),
        P("tensor"),
        P(rows, "tensor"),
    )
    return jax.shard_map(
        body,
        mesh=split,
        in_specs=placed,
        out_specs=(P(rows, "tensor"), P(rows, "tensor"), P()),
        check_vma=False,
    )
```

time: 257 us -> 233 us (0.907)
  Pallas kernels: 208 us -> 188 us
    pallas_call x3, Pallas kernels: 208 us -> 188 us  [the longest x1 103 us: gather(): pl.pallas_call(functools.partial(gather_kernel, sizes), name='gather', ou...]
    dot_general x1, matrix products: 2.77 us -> 5.41 us  [body(): jnp.einsum('tr,tf->rf', all_tokens, chain_grad, preferred_element_type=jn...]
    dot_general x1 -> x2, matrix products: 5.32 us -> 3.12 us  [body(): jnp.einsum('hrf,fk->hrk', signed[:, half], member, precision=lax.Precisio...]
where the time goes in v3:
time: 233 us; the launch traced here: 232 us
  Pallas kernels  188 us (81%)
  matrix products  33.7 us (14%)
  local copies, waits for them, and re-layouts  3.96 us (2%)
  other arithmetic  3.55 us (2%)
  between operations  3.16 us (1%)
    pallas_call x1, Pallas kernels, gather(): pl.pallas_call(functools.partial(gather_kernel, sizes), name='gather', ou...  103 us
    pallas_call x1, Pallas kernels, exchange(): pl.pallas_call(functools.partial(residual_kernel, sizes, cores), name='re...  65.8 us
    pallas_call x1, Pallas kernels, reduce_rows(): pl.pallas_call(functools.partial(reduce_kernel, sizes), name='reduce_rows...  18.9 us
    dot_general x1, matrix products, body(): jnp.einsum('ntd,df->ntf', residual, down_full, preferred_element_type=jnp...  7.1 us
    dot_general x1, matrix products, body(): tangent = jnp.dot(all_tokens, signs, preferred_element_type=jnp.float32)  5.89 us
    dot_general x1, matrix products, body(): jnp.einsum('tr,tf->rf', all_tokens, chain_grad, preferred_element_type=jn...  5.41 us

profile of v3, /device:TPU:0, one launch (start us, length us, event | category | flops | bytes accessed | tf_op | source)
XLA Modules:
  0.0 232.2 jit_solution(17039302606187750900)
XLA Ops:
  0.6 0.0 copy-start
  0.6 103.1 %gather.1 = (bf16[2,2,128,1792]{3,2,1,0:T(8,128)(2,1)}, bf16[2,2,2,2,112,896]{5,4,3,2,1,0:T(8,128)(2,1)}, bf16[2,2,2,2,112,896]{5,4,3,2,1,0:T(8,128)(2,1)}) custom-call(bf16[128,1792]{1,0:T(8,128)(2,1)} %tok_ref.1, bf16[112,3584]{1,0:T(8,128)(2,1)} %up_ref.1, bf16[112,3584]{1,0:T(8,128)(2,1)} %down_ref.1), custom_call_target="tpu_custom_call" | custom-call | tf_op jit(solution)/shard_map/gather/pallas_call | solution.py:178
  103.7 0.8 dynamic_slice.9
  104.5 0.7 broadcast_multiply_fusion
  105.2 4.6 %fusion.72 = f32[512,896]{1,0:T(8,128)S(1)} fusion(bf16[512,1792]{1,0:T(8,128)(2,1)} %bitcast.70, bf16[1792,896]{1,0:T(8,128)(2,1)} %bitcast.69), kind=kOutput, calls=%fused_computation.96 | convolution fusion | flops 1644167168 | bytes 6881280 | tf_op jit(solution)/shard_map/dot_general | solution.py:424
  109.9 5.9 %multiply_convert_fusion = (bf16[512,896]{1,0:T(8,128)(2,1)S(1)}, f32[512,896]{1,0:T(8,128)}) fusion(f32[512,896]{1,0:T(8,128)S(1)} %fusion.72, bf16[512,1792]{1,0:T(8,128)(2,1)S(1)} %bitcast.71, s32[896]{0:T(1024)S(1)} %dynamic_slice.9, s32[1792]{0:T(1024)S(1)} %broadcast_multiply_fusion), kind=kOutput, calls=%fused_computation.32 | convolution fusion | flops 1680179200 | bytes 6433280 | tf_op jit(solution)/shard_map/dot_general | solution.py:425
  115.8 3.6 %convolution_convert_fusion = bf16[512,1792]{1,0:T(8,128)(2,1)} fusion(bf16[1792,896]{1,0:T(8,128)(2,1)S(1)} %bitcast.67, f32[512,896]{1,0:T(8,128)S(1)} %fusion.72), kind=kOutput, calls=%fused_computation.15 | convolution fusion | flops 1649213440 | bytes 6881280 | tf_op jit(solution)/shard_map/dot_general | solution.py:430
  119.4 3.9 %fusion.73.dir_ref = f32[4,2,64,1792]{3,2,1,0:T(8,128)} fusion(bf16[4,2,64,896]{3,2,1,0:T(8,128)(2,1)S(1)} %bitcast.73, bf16[1792,896,1,1]{1,0,3,2:T(8,128)(2,1)S(1)} %bitcast.68), kind=kOutput, calls=%fused_computation.97 | convolution fusion | flops 1644167168 | bytes 7798784 | tf_op jit(solution)/shard_map/dot_general | solution.py:431
  123.4 0.7 constant_dynamic-slice_fusion.targets_ref
  124.1 0.1 convert_bitcast_fusion
  124.1 0.7 copy.11.live_ref
  124.9 65.8 %residual.1 = (bf16[2,4,2,64,1792]{4,3,2,1,0:T(8,128)(2,1)}, f32[4,2,8,128]{3,2,1,0:T(8,128)}) custom-call(bf16[4,2,64,1792]{3,2,1,0:T(8,128)(2,1)} %bitcast.63, f32[4,2,64,1792]{3,2,1,0:T(8,128)} %fusion.73.dir_ref, bf16[64,1792]{1,0:T(8,128)(2,1)} %constant_dynamic-slice_fusion.targets_ref, f32[64,1]{1,0:T(8,128)} %copy.11.live_ref), custom_call_target="tpu_custom_call" | custom-call | tf_op jit(solution)/shard_map/residual/pallas_call | solution.py:310
  190.7 7.1 %fusion.74 = f32[2,512,896]{2,1,0:T(8,128)S(1)} fusion(bf16[2,512,1792]{2,1,0:T(8,128)(2,1)} %bitcast.65, bf16[1792,896,1]{1,0,2:T(8,128)(2,1)} %bitcast.66), kind=kOutput, calls=%fused_computation.98 | convolution fusion | flops 3288334336 | bytes 10551296 | tf_op jit(solution)/shard_map/ntd,df->ntf/dot_general | solution.py:436
  197.8 5.4 %convert_multiply_fusion = f32[1792,896]{1,0:T(8,128)S(1)} fusion(bf16[512,1792]{1,0:T(8,128)(2,1)S(1)} %bitcast.72, s32[896]{0:T(1024)S(1)} %dynamic_slice.9, s32[1792]{0:T(1024)S(1)} %broadcast_multiply_fusion, f32[512,896]{1,0:T(8,128)S(1)} %copy-done.9, f32[2,512,896]{2,1,0:T(8,128)S(1)} %fusion.74, f32[512,896]{1,0:T(8,128)S(1)} %copy-done.8), kind=kOutput, calls=%fused_computation.8 | convolution fusion | flops 1688436736 | bytes 15608320 | tf_op jit(solution)/shard_map/tr,tf->rf/dot_general | solution.py:438
  203.3 1.2 fusion.6
  204.4 1.9 fusion.20
  206.4 0.6 reduce_sum.9.tile_ref
  207.0 18.9 %reduce_rows.1 = (f32[2,2,56,128]{3,2,1,0:T(8,128)}, f32[8,128]{1,0:T(8,128)}) custom-call(f32[2,2,2,2,56,128]{5,4,3,2,1,0:T(8,128)} %bitcast.62, f32[8,128]{1,0:T(8,128)} %reduce_sum.9.tile_ref), custom_call_target="tpu_custom_call" | custom-call | tf_op jit(solution)/shard_map/reduce_rows/pallas_call | solution.py:392
  225.9 1.3 fusion.71
  227.2 1.5 multiply_divide_fusion
  228.7 0.2 div.30
  228.9 0.1 copy.14
  229.0 0.2 div.32
  229.2 0.7 fusion.44
  (21 shorter events, 0.1 us)
Async XLA Ops:
  0.6 122.7 %copy-start = (bf16[128,1792]{1,0:T(8,128)(2,1)S(1)}, bf16[128,1792]{1,0:T(8,128)(2,1)}, u32[]{:S(2)}) copy-start(bf16[128,1792]{1,0:T(8,128)(2,1)} %param.9) | copy-start | bytes 1376260
  105.2 4.7 %copy-start.5 = (bf16[2,2,128,1792]{3,2,1,0:T(8,128)(2,1)S(1)}, bf16[2,2,128,1792]{3,2,1,0:T(8,128)(2,1)}, u32[]{:S(2)}) copy-start(bf16[2,2,128,1792]{3,2,1,0:T(8,128)(2,1)} %get-tuple-element.10) | copy-start | bytes 5505028
  109.9 5.9 %copy-start.7 = (f32[512,896]{1,0:T(8,128)}, f32[512,896]{1,0:T(8,128)S(1)}, u32[]{:S(2)}) copy-start(f32[512,896]{1,0:T(8,128)S(1)} %fusion.72) | copy-start | bytes 5505028
  109.9 5.9 %copy-start.4 = (bf16[2,2,2,2,112,896]{5,4,3,2,1,0:T(8,128)(2,1)S(1)}, bf16[2,2,2,2,112,896]{5,4,3,2,1,0:T(8,128)(2,1)}, u32[]{:S(2)}) copy-start(bf16[2,2,2,2,112,896]{5,4,3,2,1,0:T(8,128)(2,1)} %get-tuple-element.12) | copy-start | bytes 9633796
  119.4 4.6 %copy-start.6 = (s32[128]{0:T(128)S(1)}, s32[128]{0:T(128)}, u32[]{:S(2)}) copy-start(s32[128]{0:T(128)} %param.10) | copy-start | bytes 1540
  190.7 7.1 %copy-start.8 = (f32[512,896]{1,0:T(8,128)S(1)}, f32[512,896]{1,0:T(8,128)}, u32[]{:S(2)}) copy-start(f32[512,896]{1,0:T(8,128)} %copy-done.7) | copy-start | bytes 5505028
  190.7 7.1 %copy-start.9 = (f32[512,896]{1,0:T(8,128)S(1)}, f32[512,896]{1,0:T(8,128)}, u32[]{:S(2)}) copy-start(f32[512,896]{1,0:T(8,128)} %get-tuple-element.20) | copy-start | bytes 5505028
  203.2 3.2 %copy-start.3 = (f32[4,2,8,128]{3,2,1,0:T(8,128)S(1)}, f32[4,2,8,128]{3,2,1,0:T(8,128)}, u32[]{:S(2)}) copy-start(f32[4,2,8,128]{3,2,1,0:T(8,128)} %get-tuple-element.14) | copy-start | bytes 98308
  204.4 24.7 %copy-start.2 = (f32[112,256]{1,0:T(8,128)S(1)}, f32[112,256]{1,0:T(8,128)}, u32[]{:S(2)}) copy-start(f32[112,256]{1,0:T(8,128)} %param.15) | copy-start | bytes 344068
  229.2 1.9 copy-start.1

commit v4 on v3

--- a/solution.py
+++ b/solution.py
@@ -63,7 +63,7 @@
 
 def gather_kernel(
     sizes, tok_ref, up_ref, down_ref, tok_all, up_all, down_all,
-    own_sem, tok_send, tok_recv, swap_send, swap_recv, far_send, far_recv, near_send, near_recv,
+    own_sem, tok_send, tok_recv, pass_send, pass_recv, swap_send, swap_recv, far_send, far_recv, near_send, near_recv,
 ):
     na, nb, ne, nf = sizes
     a, b, e, f, c = (lax.axis_index(name) for name in AXES)
@@ -82,6 +82,8 @@
 
     friends = [peer(d, 1) for d in range(1, len(plane))]
     friends += [far(s, 1) for s in range(1, na)] + [near(t, 1) for t in range(1, ne)]
+    twin = (a, b, e, f, 1 - c)
+    friends.append(twin)
     for place in friends:
         pl.semaphore_signal(barrier, inc=1, device_id=place, device_id_type=MESH)
     pl.semaphore_wait(barrier, len(friends))
@@ -103,8 +105,13 @@
 
     def token(d, way):
         place = peer(d, way)
-        slot = tok_all.at[b, f] if way > 0 else tok_all.at[place[1], place[3]]
-        return remote(tok_ref, slot, tok_send.at[d - 1], tok_recv.at[d - 1], place)
+        slot = tok_all.at[b, f, c] if way > 0 else tok_all.at[place[1], place[3], c]
+        return remote(tok_ref.at[c], slot, tok_send.at[d - 1], tok_recv.at[d - 1], place)
+
+    def token_pass(d, core):
+        came = peer(d, -1)
+        slot = tok_all.at[came[1], came[3], core]
+        return remote(slot, slot, pass_send.at[d - 1], pass_recv.at[d - 1], twin)
 
     def chunk(w, d, at_a, at_e):
         came = peer(d, -1)
@@ -141,6 +148,9 @@
 
             for t in range(1, ne):
                 near_hop(w, d, 0, t, 1).start()
+    for d in range(1, len(plane)):
+        token(d, -1).wait_recv()
+        token_pass(d, c).start()
     for w in range(2):
         for d in range(len(plane)):
             @pl.loop(1, na)
@@ -151,7 +161,8 @@
 
     owns[2].wait()
     for d in range(1, len(plane)):
-        token(d, -1).wait_recv()
+        token_pass(d, 1 - c).wait_recv()
+        token_pass(d, c).wait_send()
         token(d, 1).wait_send()
     for w in range(2):
         for d in range(1, len(plane)):
@@ -170,7 +181,6 @@
 
 def gather(sizes, tokens, up_weight, down_weight):
     na, nb, ne, nf = sizes
-    tok_count, features = tokens.shape
     own_rows, ff_held = up_weight.shape
     groups = nb * nf
     full = jax.ShapeDtypeStruct(sizes + (own_rows, ff_held // groups), up_weight.dtype)
@@ -178,11 +188,11 @@
     return pl.pallas_call(
         functools.partial(gather_kernel, sizes),
         name="gather",
-        out_shape=(jax.ShapeDtypeStruct((nb, nf, tok_count, features), tokens.dtype), full, full),
+        out_shape=(jax.ShapeDtypeStruct((nb, nf) + tokens.shape, tokens.dtype), full, full),
         in_specs=[ANY] * 3,
         out_specs=(ANY,) * 3,
         scratch_shapes=[
-            dma((3,)), dma((groups - 1,)), dma((groups - 1,)), dma((2, groups - 1)), dma((2, groups - 1)),
+            dma((3,)), *[dma((groups - 1,))] * 4, dma((2, groups - 1)), dma((2, groups - 1)),
             dma((2, groups, na - 1)), dma((2, groups, na - 1)),
             dma((2, groups, na, ne - 1)), dma((2, groups, na, ne - 1)),
         ],
@@ -417,7 +427,7 @@
     first = lax.axis_index("tensor") * share
     live_own = lax.dynamic_slice_in_dim(live_mask, first, share).astype(jnp.float32)[:, None]
     targets_own = lax.dynamic_slice_in_dim(targets, first, share)
-    all_tokens, up_full, down_full = gather(sizes, tokens, up_weight, down_weight)
+    all_tokens, up_full, down_full = gather(sizes, tokens.reshape(cores, share, features), up_weight, down_weight)
     all_tokens = all_tokens.reshape(-1, features)
     up_full = up_full.reshape(features, cols)
     down_full = down_full.reshape(features, cols)

time: 233 us -> 224 us (0.961)
  Pallas kernels: 188 us -> 179 us
    pallas_call x1, Pallas kernels: 103 us -> 94.2 us  [gather(): pl.pallas_call(functools.partial(gather_kernel, sizes), name='gather', ou...]
where the time goes in v4:
time: 224 us; the launch traced here: 223 us
  Pallas kernels  179 us (80%)
  matrix products  33.7 us (15%)
  local copies, waits for them, and re-layouts  3.96 us (2%)
  other arithmetic  3.55 us (2%)
  between operations  3.16 us (1%)
    pallas_call x1, Pallas kernels, gather(): pl.pallas_call(functools.partial(gather_kernel, sizes), name='gather', ou...  94.2 us
    pallas_call x1, Pallas kernels, exchange(): pl.pallas_call(functools.partial(residual_kernel, sizes, cores), name='re...  65.8 us
    pallas_call x1, Pallas kernels, reduce_rows(): pl.pallas_call(functools.partial(reduce_kernel, sizes), name='reduce_rows...  18.9 us
    dot_general x1, matrix products, body(): jnp.einsum('ntd,df->ntf', residual, down_full, preferred_element_type=jnp...  7.1 us
    dot_general x1, matrix products, body(): tangent = jnp.dot(all_tokens, signs, preferred_element_type=jnp.float32)  5.9 us
    dot_general x1, matrix products, body(): jnp.einsum('tr,tf->rf', all_tokens, chain_grad, preferred_element_type=jn...  5.41 us
    dot_general x1, matrix products, body(): preact = jnp.dot(all_tokens, up_full, preferred_element_type=jnp.float32)  4.65 us

profile of v4, /device:TPU:0, one launch (start us, length us, event | category | flops | bytes accessed | tf_op | source)
XLA Modules:
  0.0 223.3 jit_solution(14445918410098034723)
XLA Ops:
  0.6 0.0 copy-start
  0.6 94.2 %gather.1 = (bf16[2,2,2,64,1792]{4,3,2,1,0:T(8,128)(2,1)}, bf16[2,2,2,2,112,896]{5,4,3,2,1,0:T(8,128)(2,1)}, bf16[2,2,2,2,112,896]{5,4,3,2,1,0:T(8,128)(2,1)}) custom-call(bf16[2,64,1792]{2,1,0:T(8,128)(2,1)} %bitcast.66, bf16[112,3584]{1,0:T(8,128)(2,1)} %up_ref.1, bf16[112,3584]{1,0:T(8,128)(2,1)} %down_ref.1), custom_call_target="tpu_custom_call" | custom-call | tf_op jit(solution)/shard_map/gather/pallas_call | solution.py:188
  94.9 0.8 dynamic_slice.9
  95.6 0.7 broadcast_multiply_fusion
  96.3 4.6 %fusion.72 = f32[512,896]{1,0:T(8,128)S(1)} fusion(bf16[512,1792]{1,0:T(8,128)(2,1)} %bitcast.72, bf16[1792,896]{1,0:T(8,128)(2,1)} %bitcast.71), kind=kOutput, calls=%fused_computation.96 | convolution fusion | flops 1644167168 | bytes 6881280 | tf_op jit(solution)/shard_map/dot_general | solution.py:434
  101.0 5.9 %multiply_convert_fusion = (bf16[512,896]{1,0:T(8,128)(2,1)S(1)}, f32[512,896]{1,0:T(8,128)}) fusion(f32[512,896]{1,0:T(8,128)S(1)} %fusion.72, bf16[512,1792]{1,0:T(8,128)(2,1)S(1)} %bitcast.73, s32[896]{0:T(1024)S(1)} %dynamic_slice.9, s32[1792]{0:T(1024)S(1)} %broadcast_multiply_fusion), kind=kOutput, calls=%fused_computation.32 | convolution fusion | flops 1680179200 | bytes 6433280 | tf_op jit(solution)/shard_map/dot_general | solution.py:435
  106.9 3.6 %convolution_convert_fusion = bf16[512,1792]{1,0:T(8,128)(2,1)} fusion(bf16[1792,896]{1,0:T(8,128)(2,1)S(1)} %bitcast.69, f32[512,896]{1,0:T(8,128)S(1)} %fusion.72), kind=kOutput, calls=%fused_computation.15 | convolution fusion | flops 1649213440 | bytes 6881280 | tf_op jit(solution)/shard_map/dot_general | solution.py:440
  110.6 3.9 %fusion.73.dir_ref = f32[4,2,64,1792]{3,2,1,0:T(8,128)} fusion(bf16[4,2,64,896]{3,2,1,0:T(8,128)(2,1)S(1)} %bitcast.75, bf16[1792,896,1,1]{1,0,3,2:T(8,128)(2,1)S(1)} %bitcast.70), kind=kOutput, calls=%fused_computation.97 | convolution fusion | flops 1644167168 | bytes 7798784 | tf_op jit(solution)/shard_map/dot_general | solution.py:441
  114.5 0.7 constant_dynamic-slice_fusion.targets_ref
  115.2 0.1 convert_bitcast_fusion
  115.3 0.7 copy.11.live_ref
  116.0 65.8 %residual.1 = (bf16[2,4,2,64,1792]{4,3,2,1,0:T(8,128)(2,1)}, f32[4,2,8,128]{3,2,1,0:T(8,128)}) custom-call(bf16[4,2,64,1792]{3,2,1,0:T(8,128)(2,1)} %bitcast.64, f32[4,2,64,1792]{3,2,1,0:T(8,128)} %fusion.73.dir_ref, bf16[64,1792]{1,0:T(8,128)(2,1)} %constant_dynamic-slice_fusion.targets_ref, f32[64,1]{1,0:T(8,128)} %copy.11.live_ref), custom_call_target="tpu_custom_call" | custom-call | tf_op jit(solution)/shard_map/residual/pallas_call | solution.py:320
  181.8 7.1 %fusion.74 = f32[2,512,896]{2,1,0:T(8,128)S(1)} fusion(bf16[2,512,1792]{2,1,0:T(8,128)(2,1)} %bitcast.67, bf16[1792,896,1]{1,0,2:T(8,128)(2,1)} %bitcast.68), kind=kOutput, calls=%fused_computation.98 | convolution fusion | flops 3288334336 | bytes 10551296 | tf_op jit(solution)/shard_map/ntd,df->ntf/dot_general | solution.py:446
  188.9 5.4 %convert_multiply_fusion = f32[1792,896]{1,0:T(8,128)S(1)} fusion(bf16[512,1792]{1,0:T(8,128)(2,1)S(1)} %bitcast.74, s32[896]{0:T(1024)S(1)} %dynamic_slice.9, s32[1792]{0:T(1024)S(1)} %broadcast_multiply_fusion, f32[512,896]{1,0:T(8,128)S(1)} %copy-done.9, f32[2,512,896]{2,1,0:T(8,128)S(1)} %fusion.74, f32[512,896]{1,0:T(8,128)S(1)} %copy-done.8), kind=kOutput, calls=%fused_computation.8 | convolution fusion | flops 1688436736 | bytes 15608320 | tf_op jit(solution)/shard_map/tr,tf->rf/dot_general | solution.py:448
  194.4 1.2 fusion.6
  195.6 1.9 fusion.20
  197.5 0.6 reduce_sum.9.tile_ref
  198.1 18.9 %reduce_rows.1 = (f32[2,2,56,128]{3,2,1,0:T(8,128)}, f32[8,128]{1,0:T(8,128)}) custom-call(f32[2,2,2,2,56,128]{5,4,3,2,1,0:T(8,128)} %bitcast.63, f32[8,128]{1,0:T(8,128)} %reduce_sum.9.tile_ref), custom_call_target="tpu_custom_call" | custom-call | tf_op jit(solution)/shard_map/reduce_rows/pallas_call | solution.py:402
  217.0 1.3 fusion.71
  218.3 1.5 multiply_divide_fusion
  219.8 0.2 div.30
  220.0 0.1 copy.14
  220.1 0.2 div.32
  220.3 0.7 fusion.44
  (21 shorter events, 0.1 us)
Async XLA Ops:
  0.6 113.9 %copy-start = (bf16[128,1792]{1,0:T(8,128)(2,1)S(1)}, bf16[128,1792]{1,0:T(8,128)(2,1)}, u32[]{:S(2)}) copy-start(bf16[128,1792]{1,0:T(8,128)(2,1)} %param.9) | copy-start | bytes 1376260
  96.3 4.7 %copy-start.5 = (bf16[2,2,2,64,1792]{4,3,2,1,0:T(8,128)(2,1)S(1)}, bf16[2,2,2,64,1792]{4,3,2,1,0:T(8,128)(2,1)}, u32[]{:S(2)}) copy-start(bf16[2,2,2,64,1792]{4,3,2,1,0:T(8,128)(2,1)} %get-tuple-element.10) | copy-start | bytes 5505028
  101.0 5.9 %copy-start.7 = (f32[512,896]{1,0:T(8,128)}, f32[512,896]{1,0:T(8,128)S(1)}, u32[]{:S(2)}) copy-start(f32[512,896]{1,0:T(8,128)S(1)} %fusion.72) | copy-start | bytes 5505028
  101.0 5.9 %copy-start.4 = (bf16[2,2,2,2,112,896]{5,4,3,2,1,0:T(8,128)(2,1)S(1)}, bf16[2,2,2,2,112,896]{5,4,3,2,1,0:T(8,128)(2,1)}, u32[]{:S(2)}) copy-start(bf16[2,2,2,2,112,896]{5,4,3,2,1,0:T(8,128)(2,1)} %get-tuple-element.12) | copy-start | bytes 9633796
  110.6 4.6 %copy-start.6 = (s32[128]{0:T(128)S(1)}, s32[128]{0:T(128)}, u32[]{:S(2)}) copy-start(s32[128]{0:T(128)} %param.10) | copy-start | bytes 1540
  181.8 7.1 %copy-start.8 = (f32[512,896]{1,0:T(8,128)S(1)}, f32[512,896]{1,0:T(8,128)}, u32[]{:S(2)}) copy-start(f32[512,896]{1,0:T(8,128)} %copy-done.7) | copy-start | bytes 5505028
  181.8 7.1 %copy-start.9 = (f32[512,896]{1,0:T(8,128)S(1)}, f32[512,896]{1,0:T(8,128)}, u32[]{:S(2)}) copy-start(f32[512,896]{1,0:T(8,128)} %get-tuple-element.20) | copy-start | bytes 5505028
  194.4 3.2 %copy-start.3 = (f32[4,2,8,128]{3,2,1,0:T(8,128)S(1)}, f32[4,2,8,128]{3,2,1,0:T(8,128)}, u32[]{:S(2)}) copy-start(f32[4,2,8,128]{3,2,1,0:T(8,128)} %get-tuple-element.14) | copy-start | bytes 98308
  195.6 24.7 %copy-start.2 = (f32[112,256]{1,0:T(8,128)S(1)}, f32[112,256]{1,0:T(8,128)}, u32[]{:S(2)}) copy-start(f32[112,256]{1,0:T(8,128)} %param.15) | copy-start | bytes 344068
  220.3 1.9 copy-start.1
